TPU v7x, 32 devices: a whole 2x2x4 slice. The times are simulated.
32 devices in a mesh: seq: 4 (over y, x), wt: 8 (over z, core).
Axes of the slice: x: 2, y: 2, z: 4, core: 2. Of those that a mesh axis runs over, the one named last changes fastest.
Arguments:
- tokens: bfloat16 [24576, 768], P(('wt', 'seq')), may hold values from -6 to 6
- output_cotangent: bfloat16 [24576, 768], P(('wt', 'seq')), may hold values from -6 to 6
- attention_weight: bfloat16 [768, 2304], P('wt'), may hold values from -0.21875 to 0.21875
- query_bias: bfloat16 [768], replicated, may hold values from -3 to 3
- value_bias: bfloat16 [768], replicated, may hold values from -3 to 3
- output_weight: bfloat16 [768, 768], P('wt'), may hold values from -6 to 6
- output_bias: bfloat16 [768], replicated, may hold values from -3 to 3
- first_gain: bfloat16 [768], replicated, may hold values from 0.5 to 1.5
- first_shift: bfloat16 [768], replicated, may hold values from -3 to 3
- expand_weight: bfloat16 [768, 3072], P('wt'), may hold values from -0.21875 to 0.21875
- expand_bias: bfloat16 [3072], replicated, may hold values from -3 to 3
- contract_weight: bfloat16 [3072, 768], P('wt'), may hold values from -0.109375 to 0.109375
- contract_bias: bfloat16 [768], replicated, may hold values from -3 to 3
- second_gain: bfloat16 [768], replicated, may hold values from 0.5 to 1.5
- second_shift: bfloat16 [768], replicated, may hold values from -3 to 3
- head_gate: float32 [12], replicated, may hold values from 0.5 to 1.5
- hidden_gate: float32 [768], replicated, may hold values from 0.5 to 1.5
- unit_gate: float32 [3072], replicated, may hold values from 0.5 to 1.5
- head_mask: int32 [12], replicated, may hold values 0 or 1
- hidden_mask: int32 [768], replicated, may hold values 0 or 1
- unit_mask: int32 [3072], replicated, may hold values 0 or 1
- attention_mask: int32 [8], replicated, may hold values 0 or 1
- feedforward_mask: int32 [8], replicated, may hold values 0 or 1
- continuation_lengths: int32 [8, 2], replicated, may hold values from 512 to 1536, as said below
Outputs:
- layer_output: bfloat16 [24576, 768], P(('wt', 'seq'))
- tokens_grad: float32 [24576, 768], P(('wt', 'seq'))
- attention_weight_grad: float32 [768, 2304], P('wt')
- query_bias_grad: float32 [768], P('wt')
- value_bias_grad: float32 [768], P('wt')
- output_weight_grad: float32 [768, 768], P('wt')
- output_bias_grad: float32 [768], P('wt')
- first_gain_grad: float32 [768], P('wt')
- first_shift_grad: float32 [768], P('wt')
- expand_weight_grad: float32 [768, 3072], P('wt')
- expand_bias_grad: float32 [3072], P('wt')
- contract_weight_grad: float32 [3072, 768], P('wt')
- contract_bias_grad: float32 [768], P('wt')
- second_gain_grad: float32 [768], P('wt')
- second_shift_grad: float32 [768], P('wt')
- head_gate_grad: float32 [12], replicated
- hidden_gate_grad: float32 [768], P('wt')
- unit_gate_grad: float32 [3072], P('wt')
Inputs may be any that keep to these rules, and one draw needn't show every extreme that they name: `continuation_lengths`: row g lists the lengths of group g's 2 continuations; in every row one continuation, at a place drawn from the seed, has exactly 1536 tokens, and the others share the remaining 2 * 1024 - 1536 tokens evenly, any remainder on the last of them.
All inputs are finite; a program needn't handle non-finite values.
Results may differ from a plain program's by a relative error of at most 0.018.
Values may be sent and summed in bfloat16 or wider, within the bound.
A program may use at most 192 MiB of HBM per device.

v0:
```python
import functools

import jax
import jax.numpy as jnp
from jax import lax
from jax.experimental import pallas as pl
from jax.experimental.pallas import tpu as pltpu
from jax.sharding import PartitionSpec as P

PROMPT = 1024
GRP_WT = 1
GLEN = 3072
SHORT = 512
LONG = 1536
HD = 64
TQ = 512
KC = 512

epsilon = 1e-06
score_scale = 0.125
exp2_scale = 0.125 * 1.4426950408889634
root_half = 0.7071067811865476
density_scale = 0.3989422804014327
bf16 = jnp.bfloat16
f32 = jnp.float32

NT = (((1,), (1,)), ((), ()))
NN = (((1,), (0,)), ((), ()))
TN = (((0,), (0,)), ((), ()))


def mm(a, b, dims=NN):
    return lax.dot_general(a, b, dims, preferred_element_type=f32)


def natural_at(short_first, i):
    other = jnp.where(i == 2, 5, i - 1)
    return jnp.where(short_first | (i < 2), i, other)


def ordered_at(short_first, j):
    other = jnp.where(j == 5, 2, j + 1)
    return jnp.where(short_first | (j < 2), j, other)


def query_tiles(tile):
    def prompt(i, carry):
        tile(i, ())
        return carry

    def longer(i, carry):
        tile(i, (3, 4, 5))
        return carry

    lax.fori_loop(0, 2, prompt, 0)
    tile(2, (2,))
    lax.fori_loop(3, 6, longer, 0)


def remote(src, dst, sems, k, peer):
    return pltpu.make_async_remote_copy(
        src_ref=src,
        dst_ref=dst,
        send_sem=sems[0].at[k],
        recv_sem=sems[1].at[k],
        device_id=peer,
        device_id_type=pl.DeviceIdType.MESH,
    )


def send(src, dst, sems, k, peer):
    copy = remote(src, dst, sems, k, peer)
    copy.start()
    return copy


def value_scale(head, group, kept_ref, gate_ref, mask_ref):
    return mask_ref[head].astype(f32) * gate_ref[head] * kept_ref[group].astype(f32)


def attend_kernel(
    heads, n, lens_ref, kept_ref, gate_ref, mask_ref, qb_ref, vb_ref, tok_ref, w_ref, exp_ref,
    packed_ref, ctx_ref, lse_ref, full_ref, exp_all,
    q_sc, k_sc, vt_sc, ct_sc, vec_ref, exp_buf,
    local_sem, s_sem, r_sem, s_e, r_e,
):
    s, w = lax.axis_index("seq"), lax.axis_index("wt")
    others = [flip(s, k) for k in (1, 2, 3)]
    mate = (s, flip(w, 1))
    short_first = lens_ref[w, 0] == SHORT
    come = pltpu.make_async_copy(exp_ref, exp_buf, local_sem.at[heads])
    come.start()
    meet([(p, w) for p in others] + [mate])
    core, quarter = lax.rem(w, 2), exp_ref.shape[2]

    def exp_place(p):
        return exp_all.at[:, core, :, pl.ds(pl.multiple_of(p * quarter, 128), quarter)]

    spread = [
        send(exp_ref, exp_place(s), (s_e, r_e), k, (p, w)) for k, p in enumerate(others)
    ] + [send(exp_ref, exp_place(s), (s_e, r_e), 3, mate)]
    width = heads * HD
    count = GLEN // 4
    vec_ref[...] = jnp.zeros_like(vec_ref)
    for k in range(4):

        @pl.when(s == k)
        def _(k=k):
            query = qb_ref[...].astype(f32).reshape(1, 4 * width)
            value = vb_ref[...].astype(f32).reshape(1, 4 * width)
            for h in range(heads):
                own = slice(k * width + h * HD, k * width + (h + 1) * HD)
                at = 3 * HD * h
                vec_ref[0:1, at : at + HD] = query[:, own]
                vec_ref[0:1, at + 2 * HD : at + 3 * HD] = value[:, own]

    for h in range(heads):
        at = 3 * HD * h
        vec_ref[1:2, at : at + 2 * HD] = jnp.ones((1, 2 * HD), f32)
        scale = value_scale(s * heads + h, w, kept_ref, gate_ref, mask_ref)
        vec_ref[1:2, at + 2 * HD : at + 3 * HD] = jnp.full((1, HD), scale, f32)
    come.wait()
    own_part = pltpu.make_async_copy(exp_buf, exp_place(s), local_sem.at[heads])
    own_part.start()

    def project(i, carry):
        rows = pl.ds(pl.multiple_of(i * TQ, TQ), TQ)
        x = mm(tok_ref[natural_at(short_first, i)], w_ref[...]) + vec_ref[0:1, :]
        x = (x * vec_ref[1:2, :]).astype(bf16)
        for h in range(heads):
            at = 3 * HD * h
            packed_ref[h, rows, :] = x[:, at : at + 3 * HD]
            q_sc[h, rows, :] = x[:, at : at + HD]
            k_sc[h, rows, :] = x[:, at + HD : at + 2 * HD]
            vt_sc[h, :, rows] = x[:, at + 2 * HD : at + 3 * HD].T
        return carry

    lax.fori_loop(0, GLEN // TQ, project, 0)

    def leaving(h):
        rows = pl.ds(pl.multiple_of(h * HD, HD), HD)
        there = full_ref.at[pl.ds(pl.multiple_of(s * width + h * HD, HD), HD), :]

        def part(p):
            return ctx_ref.at[rows, pl.ds(pl.multiple_of(p * count, 128), count)]

        copies = [
            remote(part(p), there, (s_sem, r_sem), 3 * h + k, (p, w)) for k, p in enumerate(others)
        ]
        return copies, pltpu.make_async_copy(part(s), there, local_sem.at[h])

    passed = [
        (spread[k], remote(exp_place(p), exp_place(p), (s_e, r_e), 4 + k, mate))
        for k, p in enumerate(others)
    ]

    def one_head(h, carry):
        @pl.when(h == heads - 1)
        def _():
            for came, copy in passed:
                came.wait_recv()
                copy.start()

        def tile(i, own_blocks):
            rows = pl.ds(pl.multiple_of(i * TQ, TQ), TQ)
            q = q_sc[h, rows, :]
            s1 = mm(k_sc[h, 0:PROMPT, :], q, NT)
            top = jnp.max(s1, axis=0, keepdims=True)
            if own_blocks:
                own = slice(own_blocks[0] * KC, (own_blocks[-1] + 1) * KC)
                s2 = mm(k_sc[h, own, :], q, NT)
                top = jnp.maximum(top, jnp.max(s2, axis=0, keepdims=True))
            top = top * exp2_scale
            p1 = jnp.exp2(s1 * exp2_scale - top)
            o = mm(vt_sc[h, :, 0:PROMPT], p1.astype(bf16))
            total = jnp.sum(p1, axis=0, keepdims=True)
            if own_blocks:
                p2 = jnp.exp2(s2 * exp2_scale - top)
                o = o + mm(vt_sc[h, :, own], p2.astype(bf16))
                total = total + jnp.sum(p2, axis=0, keepdims=True)
            ct_sc[i] = (o / total).astype(bf16)
            lse_ref[h, :, rows] = top + jnp.log2(total)

        query_tiles(tile)

        def settle(j, carry):
            rows = pl.ds(pl.multiple_of(h * HD, HD), HD)
            lanes = pl.ds(pl.multiple_of(j * SHORT, SHORT), SHORT)
            ctx_ref[rows, lanes] = ct_sc[ordered_at(short_first, j)]
            return carry

        lax.fori_loop(0, GLEN // SHORT, settle, 0)
        copies, own = leaving(h)
        for copy in copies:
            copy.start()
        own.start()
        return carry

    lax.fori_loop(0, heads, one_head, 0)
    own_part.wait()
    spread[3].wait_recv()
    for _, copy in passed:
        copy.wait()
    for copy in spread:
        copy.wait_send()
    for h in range(heads):
        copies, own = leaving(h)
        own.wait()
        for copy in copies:
            copy.wait()


def attend(n, lens, kept, gate, mask, query_bias, value_bias, tokens_all, weight, exp_part, heads):
    width = 3 * HD * heads
    return pl.pallas_call(
        functools.partial(attend_kernel, heads, n),
        out_shape=(
            jax.ShapeDtypeStruct((heads, GLEN, 3 * HD), bf16),
            jax.ShapeDtypeStruct((HD * heads, GLEN), bf16),
            jax.ShapeDtypeStruct((heads, 1, GLEN), f32),
            jax.ShapeDtypeStruct((4 * HD * heads, GLEN // 4), bf16),
            jax.ShapeDtypeStruct((n // 2, 2, exp_part.shape[1], 4 * exp_part.shape[2]), bf16),
        ),
        in_specs=[IN_SMEM] * 4 + [IN_VMEM] * 4 + [ANYWHERE],
        out_specs=(IN_VMEM, IN_VMEM, IN_VMEM, ANYWHERE, ANYWHERE),
        scratch_shapes=[
            pltpu.VMEM((heads, GLEN, HD), bf16),
            pltpu.VMEM((heads, GLEN, HD), bf16),
            pltpu.VMEM((heads, HD, GLEN), bf16),
            pltpu.VMEM((GLEN // TQ, HD, TQ), bf16),
            pltpu.VMEM((2, width), f32),
            pltpu.VMEM(exp_part.shape, bf16),
            pltpu.SemaphoreType.DMA((heads + 1,)),
        ]
        + dma_sems(3 * heads)
        + dma_sems(7),
        compiler_params=remote_params(1),
        cost_estimate=pl.CostEstimate(
            flops=2 * GLEN * 768 * width + heads * 4 * 256 * 5767168,
            bytes_accessed=2 * GLEN * (768 + width),
            transcendentals=heads * 5767168,
        ),
        name="attend",
    )(
        lens, kept, gate, mask, query_bias, value_bias,
        tokens_all.reshape(GLEN // TQ, TQ, -1), weight, exp_part,
    )


def attend_back_kernel(
    heads, n, lens_ref, kept_ref, gate_ref, mask_ref, packed_hbm, ctx_ref, g_hbm, lse_ref, tok_hbm,
    e_hbm, o_hbm, pieces_o, dw_o, exp_o, out_o, late_o,
    packed_v, tok_v, e_own, o_own, e_got, o_got, e_all, o_all, e_sum, o_sum, e_z, o_z, gh0, gh1, gh2, stage, late_sc,
    q_sc, k_sc, v_sc, kt_sc, g_sc, g_nat, delta_sc, delta_nat, dqt_sc, dk_sc, dv_sc, acc,
    l_in, l_g, l_out, s_g, r_g, s_p, r_p, s_c, r_c, s_e, r_e, s_z, r_z,
):
    s, w = lax.axis_index("seq"), lax.axis_index("wt")
    others = [flip(s, k) for k in (1, 2, 3)]
    mate = (s, flip(w, 1))
    z, c, nz = w // 2, lax.rem(w, 2), n // 2
    far = [lax.rem(z + j, nz) for j in range(1, nz)]
    short_first = lens_ref[w, 0] == SHORT
    count = GLEN // 4
    width = heads * HD
    gh = (gh0, gh1, gh2)[:heads]
    loads = [
        pltpu.make_async_copy(packed_hbm.at[h], packed_v.at[h], l_in.at[h]) for h in range(heads)
    ] + [
        pltpu.make_async_copy(e_hbm.at[c], e_own, l_in.at[heads]),
        pltpu.make_async_copy(o_hbm.at[c], o_own, l_in.at[heads + 1]),
        pltpu.make_async_copy(tok_hbm, tok_v, l_in.at[heads + 2]),
    ]
    for copy in loads:
        copy.start()
    meet([(p, w) for p in others] + [mate] + [(s, 2 * k + c) for k in far])

    def coming(h, own=False):
        def part(p):
            return g_hbm.at[pl.ds(pl.multiple_of(p * width + h * HD, HD), HD), :]

        there = gh[h].at[:, pl.ds(pl.multiple_of(s * count, 128), count)]
        if own:
            return pltpu.make_async_copy(part(s), there, l_g.at[h])
        return [remote(part(p), there, (s_g, r_g), 3 * h + k, (p, w)) for k, p in enumerate(others)]

    def leaving(h, own=False):
        if own:
            return pltpu.make_async_copy(stage.at[h, s], pieces_o.at[h, s], l_out.at[h])
        return [
            remote(stage.at[h, p], pieces_o.at[h, s], (s_p, r_p), 3 * h + k, (p, w))
            for k, p in enumerate(others)
        ]

    over_pair = [
        remote(e_hbm.at[1 - c], e_got, (s_c, r_c), 0, mate),
        remote(o_hbm.at[1 - c], o_got, (s_c, r_c), 1, mate),
    ]
    over_plane = [
        remote(e_got.at[p], e_all.at[s], (s_e, r_e), k, (p, w)) for k, p in enumerate(others)
    ] + [remote(o_got.at[p], o_all.at[s], (s_e, r_e), 3 + k, (p, w)) for k, p in enumerate(others)]
    over_z = [
        remote(e_sum.at[k], e_z.at[z], (s_z, r_z), j, (s, 2 * k + c)) for j, k in enumerate(far)
    ] + [
        remote(o_sum.at[k], o_z.at[z], (s_z, r_z), nz - 1 + j, (s, 2 * k + c))
        for j, k in enumerate(far)
    ]
    for h in range(heads):
        for copy in coming(h) + [coming(h, True)]:
            copy.start()
        if h == 0:
            for copy in over_pair:
                copy.start()
    late_sc[...] = jnp.zeros_like(late_sc)

    def prologue(h):
        pltpu.make_async_copy(packed_hbm.at[h], packed_v.at[h], l_in.at[h]).wait()

        def split(i, carry):
            rows = pl.ds(pl.multiple_of(i * TQ, TQ), TQ)
            x = packed_v[h, rows, :]
            q_sc[i] = x[:, 0:HD]
            k = x[:, HD : 2 * HD]
            k_sc[i] = k
            kt_sc[i] = k.T
            v_sc[i] = x[:, 2 * HD : 3 * HD]
            return carry

        lax.fori_loop(0, GLEN // TQ, split, 0)
        dk_sc[...] = jnp.zeros_like(dk_sc)
        dv_sc[...] = jnp.zeros_like(dv_sc)
        for j in range(heads):

            @pl.when(h == j)
            def _(j=j):
                coming(j, True).wait()
                for copy in coming(j):
                    copy.wait_recv()

                def take(i, carry):
                    g_nat[i] = gh[j][:, pl.ds(pl.multiple_of(i * TQ, TQ), TQ)]
                    return carry

                lax.fori_loop(0, GLEN // TQ, take, 0)

        def inner(i, carry):
            lanes = pl.ds(pl.multiple_of(i * TQ, TQ), TQ)
            ctx = ctx_ref[pl.ds(pl.multiple_of(h * HD, HD), HD), lanes]
            product = g_nat[i].astype(f32) * ctx.astype(f32)
            delta_nat[i] = jnp.sum(product, axis=0, keepdims=True)
            return carry

        def order(i, carry):
            g_sc[i] = g_nat[natural_at(short_first, i)]
            delta_sc[i] = delta_nat[natural_at(short_first, i)]
            return carry

        lax.fori_loop(0, GLEN // TQ, inner, 0)
        lax.fori_loop(0, GLEN // TQ, order, 0)

    def halfway(h):
        if h == 0:
            loads[heads].wait()
            loads[heads + 1].wait()
            for copy in over_pair:
                copy.wait_recv()

            def pair_sum(i, carry):
                q, k = i // nz, lax.rem(i, nz)
                e_got[q, k] = (e_got[q, k].astype(f32) + e_own[q, k].astype(f32)).astype(bf16)
                o_got[q, k] = (o_got[q, k].astype(f32) + o_own[q, k].astype(f32)).astype(bf16)
                return carry

            lax.fori_loop(0, 4 * nz, pair_sum, 0)
            for copy in over_plane:
                copy.start()
            e_all[s] = e_got[s]
            o_all[s] = o_got[s]
        if h == heads - 1:
            for copy in over_plane:
                copy.wait_recv()

            def add4(ref, k):
                t = [ref[q, k].astype(f32) for q in range(4)]
                return ((t[0] + t[1]) + (t[2] + t[3])).astype(bf16)

            def plane_sum(k, carry):
                e_sum[k] = add4(e_all, k)
                o_sum[k] = add4(o_all, k)
                return carry

            lax.fori_loop(0, nz, plane_sum, 0)
            for copy in over_z:
                copy.start()
            e_z[z] = e_sum[z]
            o_z[z] = o_sum[z]

    def epilogue(h, first, last):
        half = SHORT // 2
        scale = value_scale(s * heads + h, w, kept_ref, gate_ref, mask_ref)

        def settle(j, carry):
            i = ordered_at(short_first, j)
            dq = dqt_sc[i].astype(bf16)
            dk = (dk_sc[i] * score_scale).T.astype(bf16)
            dv = dv_sc[i].T.astype(bf16).astype(f32)
            gate = dv * v_sc[i].T.astype(f32)
            dv = (dv * scale).astype(bf16)
            for row, x in ((0, dq.astype(f32)), (HD, dv.astype(f32)), (2 * HD, gate)):
                x = (x[:, 0:128] + x[:, 128:256]) + (x[:, 256:384] + x[:, 384:512])
                late_sc[h, row : row + HD, :] += x
            for r in range(2):
                u = 2 * j + r
                p, there = u // 3, pl.ds(pl.multiple_of(lax.rem(u, 3) * half, half), half)
                cols = slice(r * half, (r + 1) * half)
                stage[h, p, 0:HD, there] = dq[:, cols]
                stage[h, p, HD : 2 * HD, there] = dk[:, cols]
                stage[h, p, 2 * HD : 3 * HD, there] = dv[:, cols]
            return carry

        lax.fori_loop(first, last, settle, 0)
        for p, copy in zip(others, leaving(h), strict=True):

            @pl.when(p // 2 == (0 if first == 0 else 1))
            def _(copy=copy):
                copy.start()

        if first == 0:
            leaving(h, True).start()

    def tile_of(h):
        def tile(i, own_blocks):
            q = q_sc[i]
            g = g_sc[i]
            lse = lse_ref[h, :, pl.ds(pl.multiple_of(i * TQ, TQ), TQ)]
            delta = delta_sc[i]
            dq = jnp.zeros((HD, TQ), f32)
            for j in (0, 1) + own_blocks:
                sc = mm(k_sc[j], q, NT)
                p = jnp.exp2(sc * exp2_scale - lse)
                dp = mm(v_sc[j], g)
                ds = (p * (dp - delta)).astype(bf16)
                dv_sc[j] += mm(p.astype(bf16), g, NT)
                dk_sc[j] += mm(ds, q)
                dq = dq + mm(kt_sc[j], ds)
            dqt_sc[i] = dq * score_scale

        return tile

    def one_head(h, carry):
        prologue(h)
        def longer(i, carry):
            tile_of(h)(i, (3, 4, 5))
            return carry

        def prompt(i, carry):
            tile_of(h)(i, ())
            return carry

        tile_of(h)(2, (2,))
        for j in (0, heads - 1):

            @pl.when(h == j)
            def _(j=j):
                halfway(j)

        lax.fori_loop(3, 6, longer, 0)
        epilogue(h, 2, 6)
        lax.fori_loop(0, 2, prompt, 0)
        epilogue(h, 0, 2)
        return carry

    lax.fori_loop(0, heads, one_head, 0)
    loads[heads + 2].wait()
    acc[...] = jnp.zeros_like(acc)

    def weight_grad(p, carry):
        x = tok_v[pl.ds(pl.multiple_of(p * count, count), count), :]
        for h in range(heads):
            acc[3 * HD * h : 3 * HD * (h + 1), :] += mm(stage[h, p], x)
        return carry

    lax.fori_loop(0, 4, weight_grad, 0)
    own_rows = dw_o.shape[1]
    grad = acc[...].T.astype(bf16)
    for k in range(n):
        dw_o[k] = grad[k * own_rows : (k + 1) * own_rows, :]
    late_o[...] = jnp.zeros_like(late_o)
    for h in range(heads):
        sums = jnp.sum(late_sc[h].T, axis=0, keepdims=True)
        for k in range(3):
            late_o[k : k + 1, HD * h : HD * (h + 1)] = sums[:, HD * k : HD * (k + 1)]
    for copy in over_z:
        copy.wait_recv()
    for ref, out in ((e_z, exp_o), (o_z, out_o)):
        total = ref[0].astype(f32)
        for k in range(1, nz):
            total = total + ref[k].astype(f32)
        out[...] = total.astype(bf16)
    for h in range(heads):
        for copy in [leaving(h, True)] + leaving(h):
            copy.wait()
        for copy in coming(h):
            copy.wait_send()
    for copy in over_pair + over_plane + over_z:
        copy.wait_send()


def attend_back(n, lens, kept, gate, mask, packed, ctx, g, lse, tokens_all, e_parts, o_parts):
    heads = packed.shape[0]
    width = 3 * HD * heads
    d = tokens_all.shape[1]
    count = GLEN // 4
    nz = n // 2
    own, wide = e_parts.shape[3:]
    part = o_parts.shape[4]
    blocks = GLEN // TQ
    rows64 = pltpu.VMEM((blocks, TQ, HD), bf16)
    blocks64 = pltpu.VMEM((blocks, HD, TQ), bf16)
    lanes64 = pltpu.VMEM((HD, GLEN), bf16)
    quarters = [pltpu.VMEM(e_parts.shape[1:], bf16), pltpu.VMEM(o_parts.shape[1:], bf16)]
    return pl.pallas_call(
        functools.partial(attend_back_kernel, heads, n),
        out_shape=(
            jax.ShapeDtypeStruct((heads, 4, 3 * HD, count), bf16),
            jax.ShapeDtypeStruct((n, d // n, width), bf16),
            jax.ShapeDtypeStruct((own, wide), bf16),
            jax.ShapeDtypeStruct((own, part), bf16),
            jax.ShapeDtypeStruct((8, HD * heads), f32),
        ),
        in_specs=[IN_SMEM] * 4
        + [ANYWHERE, IN_VMEM, ANYWHERE, IN_VMEM, ANYWHERE]
        + [ANYWHERE] * 2,
        out_specs=(ANYWHERE, IN_VMEM, IN_VMEM, IN_VMEM, IN_VMEM),
        scratch_shapes=[
            pltpu.VMEM(packed.shape, bf16),
            pltpu.VMEM(tokens_all.shape, bf16),
        ]
        + quarters * 3
        + [pltpu.VMEM((nz, own, wide), bf16), pltpu.VMEM((nz, own, part), bf16)] * 2
        + [lanes64] * 3
        + [pltpu.VMEM((heads, 4, 3 * HD, count), bf16), pltpu.VMEM((heads, 3 * HD, 128), f32)]
        + [
            rows64,
            rows64,
            rows64,
            blocks64,
            blocks64,
            blocks64,
            pltpu.VMEM((blocks, 1, TQ), f32),
            pltpu.VMEM((blocks, 1, TQ), f32),
            pltpu.VMEM((blocks, HD, TQ), f32),
            pltpu.VMEM((blocks, TQ, HD), f32),
            pltpu.VMEM((blocks, TQ, HD), f32),
            pltpu.VMEM((width, d), f32),
            pltpu.SemaphoreType.DMA((heads + 3,)),
            pltpu.SemaphoreType.DMA((heads,)),
            pltpu.SemaphoreType.DMA((heads,)),
        ]
        + dma_sems(3 * heads)
        + dma_sems(3 * heads)
        + dma_sems(2)
        + dma_sems(6)
        + dma_sems(2 * nz - 2),
        compiler_params=remote_params(2),
        cost_estimate=pl.CostEstimate(
            flops=heads * 10 * 256 * 5767168 + 2 * GLEN * d * width,
            bytes_accessed=2 * GLEN * (3 * width + d),
            transcendentals=heads * 5767168,
        ),
        name="attend_back",
    )(lens, kept, gate, mask, packed, ctx, g, lse, tokens_all, e_parts, o_parts)


def meet(peers):
    barrier = pltpu.get_barrier_semaphore()
    for peer in peers:
        pl.semaphore_signal(barrier, inc=1, device_id=peer, device_id_type=pl.DeviceIdType.MESH)
    pl.semaphore_wait(barrier, len(peers))


def flip(index, bits):
    for bit in (1, 2):
        if bits & bit:
            index = index + bit - 2 * bit * ((index // bit) % 2)
    return index


def remote_params(number):
    return pltpu.CompilerParams(
        collective_id=number, has_side_effects=True, vmem_limit_bytes=56 * 2**20
    )


ANYWHERE = pl.BlockSpec(memory_space=pl.ANY)
IN_VMEM = pl.BlockSpec(memory_space=pltpu.VMEM)
IN_SMEM = pl.BlockSpec(memory_space=pltpu.SMEM)


def dma_sems(count):
    return [pltpu.SemaphoreType.DMA((count,)), pltpu.SemaphoreType.DMA((count,))]


def gather_kernel(
    n, tok_ref, weight_ref, exp_ref, tok_all, cols_all, exp_all, tok_buf, cols_buf, exp_buf,
    local_sem, s_tok, r_tok, s_w, r_w, s_f, r_f, s_e, r_e,
):
    s, w = lax.axis_index("seq"), lax.axis_index("wt")
    rows = tok_ref.shape[0]
    half = rows // 2
    wide = cols_buf.shape[1]
    for k in range(4):

        @pl.when(s == k)
        def _(k=k):
            cols_buf[...] = weight_ref[:, k * wide : (k + 1) * wide]

    by_x, by_y, mate = (flip(s, 1), w), (flip(s, 2), w), (s, flip(w, 1))
    far = [(s, lax.rem(w + 2 * j, n)) for j in range(1, n // 2)]
    quarter = exp_buf.shape[1]
    exp_own = exp_ref.at[:, pl.ds(pl.multiple_of(s * quarter, 128), quarter)]
    come = [
        pltpu.make_async_copy(tok_ref, tok_buf, local_sem.at[0]),
        pltpu.make_async_copy(exp_own, exp_buf, local_sem.at[2]),
    ]
    for copy in come:
        copy.start()
    meet([by_x, by_y, mate] + far)

    def part(owner, k):
        return pl.ds(pl.multiple_of(owner * rows + k * half, half), half)

    tok = (s_tok, r_tok)
    first = [pl.ds(0, half), pl.ds(half, half)]
    x0 = send(tok_ref.at[first[0]], tok_all.at[part(s, 0)], tok, 0, by_x)
    y1 = send(tok_ref.at[first[1]], tok_all.at[part(s, 1)], tok, 1, by_y)
    x1 = send(tok_ref.at[first[1]], tok_all.at[part(s, 1)], tok, 2, by_x)
    y0 = send(tok_ref.at[first[0]], tok_all.at[part(s, 0)], tok, 3, by_y)
    held = [
        send(cols_buf, cols_all.at[w], (s_w, r_w), k, peer) for k, peer in enumerate(far + [mate])
    ]
    along = [
        send(exp_own, exp_all.at[w // 2], (s_e, r_e), k, peer) for k, peer in enumerate(far)
    ]
    for copy in come:
        copy.wait()
    own = [
        pltpu.make_async_copy(exp_buf, exp_all.at[w // 2], local_sem.at[2]),
        pltpu.make_async_copy(
            tok_buf, tok_all.at[pl.ds(pl.multiple_of(s * rows, rows), rows)], local_sem.at[0]
        ),
        pltpu.make_async_copy(cols_buf, cols_all.at[w], local_sem.at[1]),
    ]
    for copy in own:
        copy.start()
    passed = []
    for j in range(1, n // 2):
        origin = lax.rem(w + n - 2 * j, n)
        held[j - 1].wait_recv()
        passed.append(send(cols_all.at[origin], cols_all.at[origin], (s_f, r_f), j - 1, mate))
    x0.wait_recv()
    there = tok_all.at[part(flip(s, 1), 0)]
    passed.append(send(there, there, tok, 4, by_y))
    y1.wait_recv()
    there = tok_all.at[part(flip(s, 2), 1)]
    passed.append(send(there, there, tok, 5, by_x))
    for copy in own:
        copy.wait()
    for copy in [x1, y0, held[-1]] + passed + along:
        copy.wait_recv()
    for copy in [x0, x1, y0, y1] + held + passed + along:
        copy.wait_send()


def gather_in(n, tokens, attention_weight, expand_weight):
    rows, d = tokens.shape
    own, width = attention_weight.shape
    quarter = expand_weight.shape[1] // 4
    return pl.pallas_call(
        functools.partial(gather_kernel, n),
        out_shape=(
            jax.ShapeDtypeStruct((4 * rows, d), bf16),
            jax.ShapeDtypeStruct((n, own, width // 4), bf16),
            jax.ShapeDtypeStruct((n // 2, own, quarter), bf16),
        ),
        in_specs=[ANYWHERE, IN_VMEM, ANYWHERE],
        out_specs=(ANYWHERE,) * 3,
        scratch_shapes=[
            pltpu.VMEM(tokens.shape, bf16),
            pltpu.VMEM((own, width // 4), bf16),
            pltpu.VMEM((own, quarter), bf16),
            pltpu.SemaphoreType.DMA((3,)),
        ]
        + dma_sems(6)
        + dma_sems(n // 2)
        + dma_sems(n // 2 - 1)
        + dma_sems(n // 2 - 1),
        compiler_params=remote_params(0),
        name="gather_in",
    )(tokens, attention_weight, expand_weight)


def final_kernel(
    heads, n, base_hbm, pieces_hbm, w_hbm, con_ref, out_ref, att_ref, exp_ref, vec_ref, late_ref,
    tok_o, g_con, g_out, g_exp, g_att, r_vec2, r_late2,
    base_v, pieces_v, w_v, r_con, h_att, m_att, r_att, r_vec, r_late,
    l_in, *sems,
):
    s, w = lax.axis_index("seq"), lax.axis_index("wt")
    z, c = w // 2, lax.rem(w, 2)
    nz = n // 2
    others = [flip(s, k) for k in (1, 2, 3)]
    seq_peers = [(p, w) for p in others]
    mate = (s, flip(w, 1))
    wt_peers = [(s, lax.rem(w + j, n)) for j in range(1, n)]
    names = ("pair", "vec", "late", "con", "out2", "att", "vec2", "late2", "con2", "exp2", "att2")
    sem = {name: (sems[2 * k], sems[2 * k + 1]) for k, name in enumerate(names)}
    loads = [
        pltpu.make_async_copy(src, dst, l_in.at[k])
        for k, (src, dst) in enumerate(((pieces_hbm, pieces_v), (w_hbm, w_v), (base_hbm, base_v)))
    ]
    for copy in loads:
        copy.start()
    meet(seq_peers + wt_peers)
    pair = [send(att_ref.at[2 * k + 1 - c], h_att.at[k], sem["pair"], k, mate) for k in range(nz)]
    cons = [send(con_ref.at[p], r_con.at[s], sem["con"], k, (p, w)) for k, p in enumerate(others)]
    far = [lax.rem(z + j, nz) for j in range(1, nz)]
    exp2 = [send(exp_ref, g_exp.at[s], sem["exp2"], k, p) for k, p in enumerate(seq_peers)]
    out2 = [send(out_ref, g_out.at[s], sem["out2"], k, p) for k, p in enumerate(seq_peers)]
    vecs = [
        send(vec_ref.at[lax.rem(w + j, n)], r_vec.at[w], sem["vec"], j - 1, wt_peers[j - 1])
        for j in range(1, n)
    ]
    lates = [send(late_ref, r_late.at[w], sem["late"], j, p) for j, p in enumerate(wt_peers)]
    r_con[s] = con_ref[s]
    g_exp[s] = exp_ref[...]
    r_vec[w] = vec_ref[w]
    r_late[w] = late_ref[...]
    g_out[s] = out_ref[...]
    for copy in pair:
        copy.wait_recv()
    for k in range(nz):
        m_att[k] = (att_ref[2 * k + c].astype(f32) + h_att[k].astype(f32)).astype(bf16)
    atts = [send(m_att.at[k], r_att.at[z], sem["att"], j, (s, 2 * k + c)) for j, k in enumerate(far)]
    r_att[z] = m_att[z]
    for copy in loads:
        copy.wait()
    cols = 3 * HD
    rows = tok_o.shape[0]
    block = rows // 3

    def total_of(ref, count):
        total = ref[0].astype(f32)
        for k in range(1, count):
            total = total + ref[k].astype(f32)
        return total

    own = [ref.at[s] for ref in (g_con, r_vec2, r_late2, g_att)]
    con2, vec2, late2, att2 = (
        [remote(ref, ref, sem[name], k, p) for k, p in enumerate(seq_peers)]
        for ref, name in zip(own, ("con2", "vec2", "late2", "att2"), strict=True)
    )

    def tokens_block(i, carry):
        there = pl.ds(pl.multiple_of(i * block, block), block)
        total = base_v[there, :]
        for h in range(heads):
            for k in range(4):
                at = (heads * k + h) * cols
                total = total + mm(pieces_v[h, k, :, there].T, w_v[:, at : at + cols], NT)
        tok_o[there, :] = total

        @pl.when(i == 0)
        def _():
            for copy in cons:
                copy.wait_recv()
            g_con[s] = total_of(r_con, 4).astype(bf16)
            for copy in con2:
                copy.start()
            for copy in vecs + lates:
                copy.wait_recv()
            r_vec2[s] = total_of(r_vec, n)
            r_late2[s] = total_of(r_late, n)
            for copy in vec2 + late2:
                copy.start()

        @pl.when(i == 1)
        def _():
            for copy in atts:
                copy.wait_recv()
            g_att[s] = total_of(r_att, nz).astype(bf16)
            for copy in att2:
                copy.start()

        return carry

    lax.fori_loop(0, 3, tokens_block, 0)
    for copy in out2 + con2 + vec2 + late2 + exp2 + att2:
        copy.wait_recv()
    for copy in pair + cons + vecs + lates + atts + con2 + vec2 + late2 + exp2 + out2 + att2:
        copy.wait_send()


def final(n, base, pieces, weight, con, out, att, exp_part, vec, late):
    heads = pieces.shape[0]
    r, d = con.shape[1:]
    cols = att.shape[2]
    nz = n // 2
    counts = (nz, n - 1, n - 1, 3, 3, nz - 1, 3, 3, 3, 3, 3)
    return pl.pallas_call(
        functools.partial(final_kernel, heads, n),
        out_shape=(
            jax.ShapeDtypeStruct(base.shape, f32),
            jax.ShapeDtypeStruct((4, r, d), bf16),
            jax.ShapeDtypeStruct((4,) + out.shape, bf16),
            jax.ShapeDtypeStruct((4,) + exp_part.shape, bf16),
            jax.ShapeDtypeStruct((4, r, cols), bf16),
            jax.ShapeDtypeStruct((4,) + vec.shape[1:], f32),
            jax.ShapeDtypeStruct((4,) + late.shape, f32),
        ),
        in_specs=[ANYWHERE] * 3 + [IN_VMEM] * 6,
        out_specs=(IN_VMEM,) * 7,
        scratch_shapes=[
            pltpu.VMEM(base.shape, f32),
            pltpu.VMEM(pieces.shape, bf16),
            pltpu.VMEM(weight.shape, bf16),
            pltpu.VMEM((4, r, d), bf16),
            pltpu.VMEM((nz, r, cols), bf16),
            pltpu.VMEM((nz, r, cols), bf16),
            pltpu.VMEM((nz, r, cols), bf16),
            pltpu.VMEM((n,) + vec.shape[1:], f32),
            pltpu.VMEM((n,) + late.shape, f32),
            pltpu.SemaphoreType.DMA((3,)),
        ]
        + [sem for count in counts for sem in dma_sems(count)],
        compiler_params=remote_params(3),
        cost_estimate=pl.CostEstimate(
            flops=8 * base.shape[0] * d * cols, bytes_accessed=8 * d * cols, transcendentals=0
        ),
        name="final",
    )(base, pieces, weight, con, out, att, exp_part, vec, late)


def finish_kernel(n, heads, gate_ref, mask_ref, *refs):
    sources, rest = refs[:7], refs[7:]
    con_o, out_o, exp_o, att_o, tok_o = rest[:5]
    vec_os, unit_os, query_o, value_o, gate_o = rest[5:12], rest[12:14], rest[14], rest[15], rest[16]
    con_v, out_v, exp_v, att_v, vec_v, late_v, sem = rest[17:]
    loads = [
        pltpu.make_async_copy(src, dst, sem.at[k])
        for k, (src, dst) in enumerate(
            zip(sources, (con_v, out_v, exp_v, att_v, vec_v, late_v, tok_o), strict=True)
        )
    ]
    for copy in loads:
        copy.start()

    def add4(parts):
        return (parts[0] + parts[1]) + (parts[2] + parts[3])

    for copy in loads:
        copy.wait()
    wide, cols, part = exp_v.shape[2], att_v.shape[2], out_v.shape[2]
    for k in range(4):
        con_o[k] = con_v[k].astype(f32)
        exp_o[:, k * wide : (k + 1) * wide] = exp_v[k].astype(f32)
        att_o[:, k * cols : (k + 1) * cols] = att_v[k].astype(f32)
        out_o[:, k * part : (k + 1) * part] = out_v[k].astype(f32)
    vec = add4([vec_v[k] for k in range(4)])
    own = vec_os[0].shape[0]
    for k, ref in enumerate(vec_os):
        ref[...] = vec[k, 0:own]
    for k, ref in enumerate(unit_os):
        ref[...] = vec[8 + k]
    rows = [jnp.concatenate([late_v[k, j : j + 1, :] for k in range(4)], axis=1) for j in range(2)]
    for k in range(n):

        @pl.when(lax.axis_index("wt") == k)
        def _(k=k):
            query_o[...] = rows[0][0, k * own : (k + 1) * own]
            value_o[...] = rows[1][0, k * own : (k + 1) * own]

    gates = []
    for k in range(4):
        for h in range(heads):
            part_sum = jnp.sum(late_v[k, 2:3, HD * h : HD * (h + 1)], axis=1, keepdims=True)
            kept = mask_ref[heads * k + h].astype(f32) / gate_ref[heads * k + h]
            gates.append(part_sum * kept)
    gate_o[...] = jnp.concatenate(gates, axis=1)[0]


def finish(n, heads, gate, mask, con, out, exp_all, att, vec, late, tok):
    r = out.shape[1]
    wide, cols, part = exp_all.shape[2], att.shape[2], out.shape[2]
    units = vec.shape[2]
    row = jax.ShapeDtypeStruct((r,), f32)
    return pl.pallas_call(
        functools.partial(finish_kernel, n, heads),
        out_shape=(
            jax.ShapeDtypeStruct(con.shape, f32),
            jax.ShapeDtypeStruct((r, 4 * part), f32),
            jax.ShapeDtypeStruct((r, 4 * wide), f32),
            jax.ShapeDtypeStruct((r, 4 * cols), f32),
            jax.ShapeDtypeStruct(tok.shape, f32),
        )
        + (row,) * 7
        + (jax.ShapeDtypeStruct((units,), f32),) * 2
        + (row,) * 2
        + (jax.ShapeDtypeStruct((4 * heads,), f32),),
        in_specs=[IN_SMEM] * 2 + [ANYWHERE] * 7,
        out_specs=(IN_VMEM,) * 17,
        scratch_shapes=[pltpu.VMEM(x.shape, x.dtype) for x in (con, out, exp_all, att, vec, late)]
        + [pltpu.SemaphoreType.DMA((7,))],
        compiler_params=pltpu.CompilerParams(vmem_limit_bytes=56 * 2**20),
        name="finish",
    )(gate, mask, con, out, exp_all, att, vec, late, tok)


(OUT_BIAS, GAIN1, SHIFT1, HIDDEN_SCALE, CON_BIAS, GAIN2, SHIFT2, HIDDEN_MASK) = range(8)
(S_OUT_BIAS, S_GAIN1, S_SHIFT1, S_CON_BIAS, S_GAIN2, S_SHIFT2, S_HIDDEN) = range(7)


def gelu_parts(x):
    bell = jnp.exp(-0.5 * (x * x))
    t = 1.0 / (1.0 + (0.3275911 * root_half) * jnp.abs(x))
    poly = t * (
        0.127414796 + t * (-0.142248368 + t * (0.7107068705 + t * (-0.7265760135 + t * 0.5307027145)))
    )
    tail = poly * bell
    cumulative = jnp.where(x < 0.0, tail, 1.0 - tail)
    return x * cumulative, cumulative + x * bell * density_scale


def norm_parts(summed):
    centre = summed - jnp.mean(summed, axis=-1, keepdims=True)
    inverse = lax.rsqrt(jnp.mean(centre * centre, axis=-1, keepdims=True) + epsilon)
    return (centre * inverse, inverse)


def norm_back(grad_normed, normed, inverse):
    return inverse * (
        grad_normed
        - jnp.mean(grad_normed, axis=-1, keepdims=True)
        - normed * jnp.mean(grad_normed * normed, axis=-1, keepdims=True)
    )


def feed_forward_kernel(
    steps, chunk,
    kept_ref, ctx_ref, tok_ref, cot_ref, wo_ref, we_ref, wc_ref,
    ob_ref, g1_ref, t1_ref, hg_ref, hm_ref, cb_ref, g2_ref, t2_ref, eb_ref, ug_ref, um_ref,
    lo_ref, dt1_ref, gctx_ref, vec_ref, dwc_ref, dwe_ref, dwo_ref,
    wide_ref, unit_ref, sw_ref, su_ref, act_sc, gh_sc, low_sc, gb_sc, ga_sc, ctx_sc, gelu_sc, slope_sc,
):
    i = pl.program_id(0)
    block = tok_ref.shape[0]
    units = we_ref.shape[1]
    rows = pl.ds(pl.multiple_of(i * block, block), block)

    @pl.when(i == 0)
    def _():
        sw_ref[...] = jnp.zeros_like(sw_ref)
        su_ref[...] = jnp.zeros_like(su_ref)

        def row(ref):
            return ref[...].astype(f32).reshape(1, ref.shape[0])

        plain = ((OUT_BIAS, ob_ref), (GAIN1, g1_ref), (SHIFT1, t1_ref), (CON_BIAS, cb_ref))
        for k, ref in plain + ((GAIN2, g2_ref), (SHIFT2, t2_ref), (HIDDEN_MASK, hm_ref)):
            wide_ref[k : k + 1, :] = row(ref)
        wide_ref[HIDDEN_SCALE : HIDDEN_SCALE + 1, :] = row(hm_ref) * row(hg_ref)
        kept = row(um_ref) * kept_ref[lax.axis_index("wt")].astype(f32)
        unit_ref[0:1, :] = row(eb_ref)
        unit_ref[1:2, :] = kept * row(ug_ref)
        unit_ref[2:3, :] = kept

    def wide(k):
        return wide_ref[k : k + 1, :]

    def add_sum(ref, k, cols, value):
        ref[k : k + 1, cols] += jnp.sum(value, axis=0, keepdims=True)

    full = slice(None)
    ctx = ctx_ref[...]
    ctx_sc[:, rows] = ctx
    summed = mm(ctx, wo_ref[...], TN) + wide(OUT_BIAS) + tok_ref[...].astype(f32)
    n1, inv1 = norm_parts(summed)
    s1 = n1 * wide(GAIN1) + wide(SHIFT1)
    hs = wide(HIDDEN_SCALE)
    first = s1 * hs
    low = first.astype(bf16)
    low_sc[rows, :] = low
    branch = first + wide(CON_BIAS)
    for j in range(units // chunk):
        cols = slice(j * chunk, (j + 1) * chunk)
        hidden = mm(low, we_ref[:, cols]) + unit_ref[0:1, cols]
        gelu, slope = gelu_parts(hidden)
        scale = unit_ref[1:2, cols]
        gelu_sc[:, cols] = gelu.astype(gelu_sc.dtype)
        slope_sc[:, cols] = (slope * scale).astype(slope_sc.dtype)
        act = (gelu * scale).astype(bf16)
        act_sc[rows, cols] = act
        branch = branch + mm(act, wc_ref[cols, :])
    n2, inv2 = norm_parts(branch)
    s2 = n2 * wide(GAIN2) + wide(SHIFT2)
    lo_ref[...] = (s2 * hs).astype(bf16)
    dy = cot_ref[...].astype(f32)
    e2 = dy * hs
    add_sum(sw_ref, S_GAIN2, full, e2 * n2)
    add_sum(sw_ref, S_SHIFT2, full, e2)
    dt2 = norm_back(e2 * wide(GAIN2), n2, inv2)
    gb = dt2.astype(bf16)
    gb_sc[rows, :] = gb
    add_sum(sw_ref, S_CON_BIAS, full, gb.astype(f32))
    d_first = dt2
    for j in range(units // chunk):
        cols = slice(j * chunk, (j + 1) * chunk)
        d_act = mm(gb, wc_ref[cols, :], NT)
        add_sum(su_ref, 1, cols, d_act * gelu_sc[:, cols].astype(f32))
        gh = d_act * slope_sc[:, cols].astype(f32)
        add_sum(su_ref, 0, cols, gh)
        gh = gh.astype(bf16)
        gh_sc[rows, cols] = gh
        d_first = d_first + mm(gh, we_ref[:, cols], NT)
    e1 = d_first * hs
    add_sum(sw_ref, S_GAIN1, full, e1 * n1)
    add_sum(sw_ref, S_SHIFT1, full, e1)
    add_sum(sw_ref, S_HIDDEN, full, dy * s2 + d_first * s1)
    dt1 = norm_back(e1 * wide(GAIN1), n1, inv1)
    dt1_ref[...] = dt1
    ga = dt1.astype(bf16)
    ga_sc[rows, :] = ga
    add_sum(sw_ref, S_OUT_BIAS, full, ga.astype(f32))
    gctx_ref[...] = mm(wo_ref[...], ga, NT).astype(bf16)

    @pl.when(i == steps - 1)
    def _():
        own, wide_cols = dwe_ref.shape[3:]

        def weight_grads(j, carry):
            cols = pl.ds(pl.multiple_of(j * wide_cols, 128), wide_cols)
            dwc_ref[cols, :] = mm(act_sc[:, cols], gb_sc[...], TN).astype(bf16)
            part = mm(low_sc[...], gh_sc[:, cols], TN).astype(bf16)
            for k in range(2 * dwe_ref.shape[2]):
                dwe_ref[k % 2, j, k // 2] = part[k * own : (k + 1) * own]
            return carry

        lax.fori_loop(0, 4, weight_grads, 0)
        own, part_cols = dwo_ref.shape[3:]
        for q in range(4):
            part = mm(ctx_sc[...], ga_sc[:, q * part_cols : (q + 1) * part_cols]).astype(bf16)
            for k in range(2 * dwo_ref.shape[2]):
                dwo_ref[k % 2, q, k // 2] = part[k * own : (k + 1) * own]
        vec_ref[...] = jnp.zeros_like(vec_ref)
        sw_ref[S_HIDDEN : S_HIDDEN + 1, :] *= wide(HIDDEN_MASK)
        su_ref[1:2, :] *= unit_ref[2:3, :]
        own_wide, own_units = dwe_ref.shape[3], vec_ref.shape[2]
        for k in range(vec_ref.shape[0]):
            vec_ref[k, 0:8, 0:own_wide] = sw_ref[:, k * own_wide : (k + 1) * own_wide]
            vec_ref[k, 8:16, :] = su_ref[:, k * own_units : (k + 1) * own_units]


def feed_forward(n, kept, ctx_t, tokens, cotangent, wo, we, wc, *vectors):
    steps, chunk, keep = 3, 768, f32
    rows, d = tokens.shape
    units = we.shape[1]
    block = rows // steps
    halves = (2, 4, n // 2, d // n, units // 4)
    out_halves = (2, 4, n // 2, d // n, d // 4)
    tile = pl.BlockSpec((block, d), lambda i: (i, 0))
    lanes = pl.BlockSpec((d, block), lambda i: (0, i))

    def once(shape):
        return pl.BlockSpec(shape, lambda i: (0, 0), pipeline_mode=pl.Buffered(1))

    def once3(shape):
        return pl.BlockSpec(shape, lambda i: (0, 0, 0), pipeline_mode=pl.Buffered(1))

    def once5(shape):
        return pl.BlockSpec(shape, lambda i: (0, 0, 0, 0, 0), pipeline_mode=pl.Buffered(1))

    return pl.pallas_call(
        functools.partial(feed_forward_kernel, steps, chunk),
        out_shape=(
            jax.ShapeDtypeStruct((rows, d), bf16),
            jax.ShapeDtypeStruct((rows, d), f32),
            jax.ShapeDtypeStruct((d, rows), bf16),
            jax.ShapeDtypeStruct((n, 16, units // n), f32),
            jax.ShapeDtypeStruct((units, d), bf16),
            jax.ShapeDtypeStruct(halves, bf16),
            jax.ShapeDtypeStruct(out_halves, bf16),
        ),
        grid=(steps,),
        in_specs=[
            pl.BlockSpec(memory_space=pltpu.SMEM),
            lanes, tile, tile, once((d, d)), once((d, units)), once((units, d)),
        ]
        + [IN_VMEM] * len(vectors),
        out_specs=(
            tile, tile, lanes, once3((n, 16, units // n)), once((units, d)),
            once5(halves), once5(out_halves),
        ),
        scratch_shapes=[
            pltpu.VMEM((8, d), f32),
            pltpu.VMEM((8, units), f32),
            pltpu.VMEM((8, d), f32),
            pltpu.VMEM((8, units), f32),
            pltpu.VMEM((rows, units), bf16),
            pltpu.VMEM((rows, units), bf16),
            pltpu.VMEM((rows, d), bf16),
            pltpu.VMEM((rows, d), bf16),
            pltpu.VMEM((rows, d), bf16),
            pltpu.VMEM((d, rows), bf16),
            pltpu.VMEM((block, units), keep),
            pltpu.VMEM((block, units), keep),
        ],
        compiler_params=pltpu.CompilerParams(vmem_limit_bytes=60 * 2**20),
        cost_estimate=pl.CostEstimate(
            flops=rows * d * (12 * units + 6 * d),
            bytes_accessed=4 * d * (4 * units + 2 * d) + 12 * rows * d,
            transcendentals=2 * rows * units,
        ),
        name="feed_forward",
    )(kept, ctx_t, tokens, cotangent, wo, we, wc, *vectors)


def local(
    tokens,
    output_cotangent,
    attention_weight,
    query_bias,
    value_bias,
    output_weight,
    output_bias,
    first_gain,
    first_shift,
    expand_weight,
    expand_bias,
    contract_weight,
    contract_bias,
    second_gain,
    second_shift,
    head_gate,
    hidden_gate,
    unit_gate,
    head_mask,
    hidden_mask,
    unit_mask,
    attention_mask,
    feedforward_mask,
    continuation_lengths,
):
    seq_count = lax.axis_size("seq")
    wt_count = lax.axis_size("wt")
    model_width = hidden_gate.shape[0]
    local_heads = head_gate.shape[0] // seq_count
    own_wide = model_width // wt_count
    tokens_all, own_weight, exp_quarter = gather_in(wt_count, tokens, attention_weight, expand_weight)
    contract_weight, own_weight = lax.optimization_barrier((contract_weight, own_weight))
    full_contract = lax.all_gather(contract_weight, "wt", axis=0, tiled=True)
    full_attention = lax.all_gather(attention_weight, "wt", axis=0, tiled=True)
    full_output = lax.all_gather(output_weight, "wt", axis=0, tiled=True)
    packed, own_context, log_sums, context_t, full_expand = attend(
        wt_count,
        continuation_lengths,
        attention_mask,
        head_gate,
        head_mask,
        query_bias,
        value_bias,
        tokens_all,
        own_weight.reshape(model_width, -1),
        exp_quarter,
        local_heads,
    )
    (
        layer_output,
        grad_total_one,
        grad_context_t,
        vec_sums,
        contract_weight_grad,
        exp_parts,
        out_parts,
    ) = feed_forward(
        wt_count,
        feedforward_mask,
        context_t,
        tokens,
        output_cotangent,
        full_output,
        full_expand.reshape(model_width, -1),
        full_contract,
        output_bias,
        first_gain,
        first_shift,
        hidden_gate,
        hidden_mask,
        contract_bias,
        second_gain,
        second_shift,
        expand_bias,
        unit_gate,
        unit_mask,
    )
    con_piece = lax.psum_scatter(contract_weight_grad, "wt", scatter_dimension=0, tiled=True)
    pieces, projection_grad, exp_part, out_part, late_sums = attend_back(
        wt_count,
        continuation_lengths,
        attention_mask,
        head_gate,
        head_mask,
        packed,
        own_context,
        grad_context_t,
        log_sums,
        tokens_all,
        exp_parts,
        out_parts,
    )
    tokens_grad, con_all, out_all, exp_all, att_all, vec_all, late_all = final(
        wt_count,
        grad_total_one,
        pieces,
        full_attention,
        con_piece.reshape(seq_count, own_wide, model_width),
        out_part,
        projection_grad,
        exp_part,
        vec_sums,
        late_sums,
    )
    con_sum, out_sum, exp_sum, att_sum, tokens_grad, *rows = finish(
        wt_count,
        local_heads,
        head_gate,
        head_mask,
        con_all,
        out_all,
        exp_all,
        att_all,
        vec_all,
        late_all,
        tokens_grad,
    )
    return (
        layer_output,
        tokens_grad,
        att_sum,
        rows[9],
        rows[10],
        out_sum,
        rows[S_OUT_BIAS],
        rows[S_GAIN1],
        rows[S_SHIFT1],
        exp_sum,
        rows[7],
        con_sum.reshape(seq_count * own_wide, model_width),
        rows[S_CON_BIAS],
        rows[S_GAIN2],
        rows[S_SHIFT2],
        rows[11],
        rows[S_HIDDEN],
        rows[8],
    )


def solution(mesh):
    return jax.shard_map(
        local,
        mesh=mesh,
        in_specs=(
            P(("wt", "seq"), None),
            P(("wt", "seq"), None),
            P("wt", None),
            P(),
            P(),
            P("wt", None),
            P(),
            P(),
            P(),
            P("wt", None),
            P(),
            P("wt", None),
            P(),
            P(),
            P(),
            P(),
            P(),
            P(),
            P(),
            P(),
            P(),
            P(),
            P(),
            P(),
        ),
        out_specs=(
            P(("wt", "seq"), None),
            P(("wt", "seq"), None),
            P("wt", None),
            P("wt"),
            P("wt"),
            P("wt", None),
            P("wt"),
            P("wt"),
            P("wt"),
            P("wt", None),
            P("wt"),
            P("wt", None),
            P("wt"),
            P("wt"),
            P("wt"),
            P(),
            P("wt"),
            P("wt"),
        ),
        check_vma=False,
    )
```

profile of v0, /device:TPU:0, one launch (start us, length us, event | category | flops | bytes accessed | tf_op | source)
XLA Modules:
  0.0 293.2 jit_solution(6980744280191836670)
XLA Ops:
  7.2 0.0 copy-start
  7.2 0.0 all-gather.4.cloned.1.call-start
  7.2 0.7 all-gather.4.cloned.1.call-update
  7.9 0.0 all-gather.6.cloned.1.call-start
  8.0 46.7 %gather_in.1 = (bf16[3072,768]{1,0:T(8,128)(2,1)}, bf16[8,96,576]{2,1,0:T(8,128)(2,1)}, bf16[4,96,768]{2,1,0:T(8,128)(2,1)}) custom-call(bf16[768,768]{1,0:T(8,128)(2,1)} %tok_ref.3, bf16[96,2304]{1,0:T(8,128)(2,1)} %weight_ref.1, bf16[96,3072]{1,0:T(8,128)(2,1)} %exp_ref.1), custom_call_target="tpu_custom_call" | custom-call | tf_op jit(solution)/shard_map/gather_in/pallas_call | solution.py:678
  54.7 0.0 all-gather.6.cloned.1.call-update
  54.7 0.0 all-gather.8.cloned.1.call-start
  54.8 0.7 all-gather.8.cloned.1.call-update
  55.5 0.0 reduce-scatter.2.cloned.1.call-start
  55.5 0.0 copy-done
  55.5 0.7 copy.42.lens_ref
  56.2 50.9 %attend.1 = (bf16[3,3072,192]{2,1,0:T(8,128)(2,1)}, bf16[192,3072]{1,0:T(8,128)(2,1)}, f32[3,1,3072]{2,1,0:T(1,128)}, bf16[768,768]{1,0:T(8,128)(2,1)}, bf16[4,2,96,3072]{3,2,1,0:T(8,128)(2,1)}) custom-call(s32[8,2]{1,0:T(8,128)} %copy.42.lens_ref, s32[8]{0:T(128)} %kept_ref.5, f32[12]{0:T(128)} %gate_ref.5, s32[12]{0:T(128)} %mask_ref.5, ...), custom_call_target="tpu_custom_call" | custom-call | flops 20434649088 | bytes 8257536 | tf_op jit(solution)/shard_map/attend/pallas_call | solution.py:215
  107.1 0.0 all-gather.4.cloned.1.call-done.wo_ref
  107.1 0.0 all-gather.6.cloned.1.call-done.wc_ref
  107.1 47.2 %feed_forward.1 = (bf16[768,768]{1,0:T(8,128)(2,1)}, f32[768,768]{1,0:T(8,128)}, bf16[768,768]{1,0:T(8,128)(2,1)}, f32[8,16,384]{2,1,0:T(8,128)}, bf16[3072,768]...) custom-call(s32[8]{0:T(128)} %kept_ref.4, ...), custom_call_target="tpu_custom_call" | custom-call | flops 24461180928 | bytes 49545216 | tf_op jit(solution)/shard_map/feed_forward/pallas_call | solution.py:1081
  154.4 0.0 reduce-scatter.2.cloned.1.call-update
  154.4 90.8 %attend_back.1 = (bf16[3,4,192,768]{3,2,1,0:T(8,128)(2,1)}, bf16[8,96,576]{2,1,0:T(8,128)(2,1)}, bf16[96,768]{1,0:T(8,128)(2,1)}, bf16[96,192]{1,0:T(8,128)(2,1)}, f32[8,192]{1,0:T(8,128)}) custom-call(s32[8,2]{1,0:T(8,128)} %copy.42.lens_ref, s32[8]{0:T(128)} %kept_ref.5, f32[12]{0:T(128)} %gate_ref.5, s32[12]{0:T(128)} %mask_ref.5, ...), custom_call_target="tpu_custom_call" | custom-call | flops 47009759232 | bytes 15335424 | tf_op jit(solution)/shard_map/attend_back/pallas_call | solution.py:521
  245.2 0.0 all-gather.8.cloned.1.call-done.w_hbm
  245.3 0.0 reduce-scatter.2.cloned.1.call-done
  245.3 35.4 %final.1 = (f32[768,768]{1,0:T(8,128)}, bf16[4,96,768]{2,1,0:T(8,128)(2,1)}, bf16[4,96,192]{2,1,0:T(8,128)(2,1)}, bf16[4,96,768]{2,1,0:T(8,128)(2,1)}, bf16[4,96...) custom-call(f32[768,768]{1,0:T(8,128)} %get-tuple-element.72.base_hbm, ...), custom_call_target="tpu_custom_call" | custom-call | flops 2717908992 | bytes 3538944 | tf_op jit(solution)/shard_map/final/pallas_call | solution.py:809
  280.7 6.0 %finish.1 = (f32[4,96,768]{2,1,0:T(8,128)}, f32[96,768]{1,0:T(8,128)}, f32[96,3072]{1,0:T(8,128)}, f32[96,2304]{1,0:T(8,128)}, f32[768,768]{1,0:T(8,128)}, /*ind...) custom-call(f32[12]{0:T(128)} %gate_ref.5, ...), custom_call_target="tpu_custom_call" | custom-call | tf_op jit(solution)/shard_map/finish/pallas_call | solution.py:896
Async XLA Ops:
  7.2 48.3 %copy-start = (s32[8,2]{0,1:T(2,128)S(1)}, s32[8,2]{0,1:T(2,128)}, u32[]{:S(2)}) copy-start(s32[8,2]{0,1:T(2,128)} %param.47) | copy-start | bytes 196
  7.2 99.9 %all-gather.4.cloned.1.call-start = ((), (), s32[]{:S(2)}) async-start(), calls=%async_computation.1 | async-start | bytes 1327104 | tf_op jit(solution)/shard_map/all_gather | solution.py:1161
  7.9 99.2 %all-gather.6.cloned.1.call-start = ((), (), s32[]{:S(2)}) async-start(), calls=%async_computation.2 | async-start | bytes 5308416 | tf_op jit(solution)/shard_map/all_gather | solution.py:1159
  54.7 190.5 %all-gather.8.cloned.1.call-start = ((), (), s32[]{:S(2)}) async-start(), calls=%async_computation.3 | async-start | bytes 3981312 | tf_op jit(solution)/shard_map/all_gather | solution.py:1160
  55.5 189.8 %reduce-scatter.2.cloned.1.call-start = ((), (), s32[]{:S(2)}) async-start(), calls=%async_computation.4 | async-start | bytes 5308416 | tf_op jit(solution)/shard_map/reduce_scatter | solution.py:1204
Sparse Core Ops, SparseCore 0:
  9.7 35.7 all-gather.3
  54.8 49.8 all-gather.5
  106.4 40.3 all-gather.7
  154.5 53.2 reduce-scatter.1
where the time goes:
time: 293 us
  Pallas kernels  277 us (95%)
  between operations  13.9 us (5%)
    pallas_call x1, Pallas kernels, attend_back(): pl.pallas_call(functools.partial(attend_back_kernel, heads, n), out_shape...  90.8 us
    pallas_call x1, Pallas kernels, attend(): pl.pallas_call(functools.partial(attend_kernel, heads, n), out_shape=(jax...  50.9 us
    pallas_call x1, Pallas kernels, feed_forward(): pl.pallas_call(functools.partial(feed_forward_kernel, steps, chunk), out_...  47.2 us
    pallas_call x1, Pallas kernels, gather_in(): pl.pallas_call(functools.partial(gather_kernel, n), out_shape=(jax.ShapeD...  46.7 us
    pallas_call x1, Pallas kernels, final(): pl.pallas_call(functools.partial(final_kernel, heads, n), out_shape=(jax....  35.4 us
    pallas_call x1, Pallas kernels, finish(): pl.pallas_call(functools.partial(finish_kernel, n, heads), out_shape=(jax...  6.03 us
  transfers between devices with their start and end apart: 4, of which 0 were waited for; matrix products, arithmetic and copies ran while one was open for 0% of the time, Pallas kernels for 80%

commit v1 on v0

--- a/solution.py
+++ b/solution.py
@@ -248,11 +248,11 @@
 
 
 def attend_back_kernel(
-    heads, n, lens_ref, kept_ref, gate_ref, mask_ref, packed_hbm, ctx_ref, g_hbm, lse_ref, tok_hbm,
+    heads, n, lens_ref, kept_ref, gate_ref, mask_ref, packed_hbm, ctx_ref, gctx_ref, lse_ref, tok_hbm,
     e_hbm, o_hbm, pieces_o, dw_o, exp_o, out_o, late_o,
-    packed_v, tok_v, e_own, o_own, e_got, o_got, e_all, o_all, e_sum, o_sum, e_z, o_z, gh0, gh1, gh2, stage, late_sc,
+    packed_v, tok_v, e_own, o_own, e_got, o_got, e_all, o_all, e_sum, o_sum, e_z, o_z, stage, late_sc,
     q_sc, k_sc, v_sc, kt_sc, g_sc, g_nat, delta_sc, delta_nat, dqt_sc, dk_sc, dv_sc, acc,
-    l_in, l_g, l_out, s_g, r_g, s_p, r_p, s_c, r_c, s_e, r_e, s_z, r_z,
+    l_in, l_out, s_p, r_p, s_c, r_c, s_e, r_e, s_z, r_z,
 ):
     s, w = lax.axis_index("seq"), lax.axis_index("wt")
     others = [flip(s, k) for k in (1, 2, 3)]
@@ -262,7 +262,6 @@
     short_first = lens_ref[w, 0] == SHORT
     count = GLEN // 4
     width = heads * HD
-    gh = (gh0, gh1, gh2)[:heads]
     loads = [
         pltpu.make_async_copy(packed_hbm.at[h], packed_v.at[h], l_in.at[h]) for h in range(heads)
     ] + [
@@ -273,15 +272,6 @@
     for copy in loads:
         copy.start()
     meet([(p, w) for p in others] + [mate] + [(s, 2 * k + c) for k in far])
-
-    def coming(h, own=False):
-        def part(p):
-            return g_hbm.at[pl.ds(pl.multiple_of(p * width + h * HD, HD), HD), :]
-
-        there = gh[h].at[:, pl.ds(pl.multiple_of(s * count, 128), count)]
-        if own:
-            return pltpu.make_async_copy(part(s), there, l_g.at[h])
-        return [remote(part(p), there, (s_g, r_g), 3 * h + k, (p, w)) for k, p in enumerate(others)]
 
     def leaving(h, own=False):
         if own:
@@ -304,12 +294,8 @@
         remote(o_sum.at[k], o_z.at[z], (s_z, r_z), nz - 1 + j, (s, 2 * k + c))
         for j, k in enumerate(far)
     ]
-    for h in range(heads):
-        for copy in coming(h) + [coming(h, True)]:
-            copy.start()
-        if h == 0:
-            for copy in over_pair:
-                copy.start()
+    for copy in over_pair:
+        copy.start()
     late_sc[...] = jnp.zeros_like(late_sc)
 
     def prologue(h):
@@ -328,24 +314,11 @@
         lax.fori_loop(0, GLEN // TQ, split, 0)
         dk_sc[...] = jnp.zeros_like(dk_sc)
         dv_sc[...] = jnp.zeros_like(dv_sc)
-        for j in range(heads):
-
-            @pl.when(h == j)
-            def _(j=j):
-                coming(j, True).wait()
-                for copy in coming(j):
-                    copy.wait_recv()
-
-                def take(i, carry):
-                    g_nat[i] = gh[j][:, pl.ds(pl.multiple_of(i * TQ, TQ), TQ)]
-                    return carry
-
-                lax.fori_loop(0, GLEN // TQ, take, 0)
-
         def inner(i, carry):
             lanes = pl.ds(pl.multiple_of(i * TQ, TQ), TQ)
-            ctx = ctx_ref[pl.ds(pl.multiple_of(h * HD, HD), HD), lanes]
-            product = g_nat[i].astype(f32) * ctx.astype(f32)
+            own = pl.ds(pl.multiple_of(h * HD, HD), HD)
+            g_nat[i] = gctx_ref[own, lanes]
+            product = g_nat[i].astype(f32) * ctx_ref[own, lanes].astype(f32)
             delta_nat[i] = jnp.sum(product, axis=0, keepdims=True)
             return carry
 
@@ -499,8 +472,6 @@
     for h in range(heads):
         for copy in [leaving(h, True)] + leaving(h):
             copy.wait()
-        for copy in coming(h):
-            copy.wait_send()
     for copy in over_pair + over_plane + over_z:
         copy.wait_send()
 
@@ -516,7 +487,6 @@
     blocks = GLEN // TQ
     rows64 = pltpu.VMEM((blocks, TQ, HD), bf16)
     blocks64 = pltpu.VMEM((blocks, HD, TQ), bf16)
-    lanes64 = pltpu.VMEM((HD, GLEN), bf16)
     quarters = [pltpu.VMEM(e_parts.shape[1:], bf16), pltpu.VMEM(o_parts.shape[1:], bf16)]
     return pl.pallas_call(
         functools.partial(attend_back_kernel, heads, n),
@@ -528,7 +498,7 @@
             jax.ShapeDtypeStruct((8, HD * heads), f32),
         ),
         in_specs=[IN_SMEM] * 4
-        + [ANYWHERE, IN_VMEM, ANYWHERE, IN_VMEM, ANYWHERE]
+        + [ANYWHERE, IN_VMEM, IN_VMEM, IN_VMEM, ANYWHERE]
         + [ANYWHERE] * 2,
         out_specs=(ANYWHERE, IN_VMEM, IN_VMEM, IN_VMEM, IN_VMEM),
         scratch_shapes=[
@@ -537,7 +507,6 @@
         ]
         + quarters * 3
         + [pltpu.VMEM((nz, own, wide), bf16), pltpu.VMEM((nz, own, part), bf16)] * 2
-        + [lanes64] * 3
         + [pltpu.VMEM((heads, 4, 3 * HD, count), bf16), pltpu.VMEM((heads, 3 * HD, 128), f32)]
         + [
             rows64,
@@ -554,9 +523,7 @@
             pltpu.VMEM((width, d), f32),
             pltpu.SemaphoreType.DMA((heads + 3,)),
             pltpu.SemaphoreType.DMA((heads,)),
-            pltpu.SemaphoreType.DMA((heads,)),
         ]
-        + dma_sems(3 * heads)
         + dma_sems(3 * heads)
         + dma_sems(2)
         + dma_sems(6)
@@ -946,18 +913,42 @@
 
 def feed_forward_kernel(
     steps, chunk,
-    kept_ref, ctx_ref, tok_ref, cot_ref, wo_ref, we_ref, wc_ref,
+    kept_ref, ctx_ref, tok_ref, cot_ref, wo_ref, we_hbm, wc_hbm,
     ob_ref, g1_ref, t1_ref, hg_ref, hm_ref, cb_ref, g2_ref, t2_ref, eb_ref, ug_ref, um_ref,
-    lo_ref, dt1_ref, gctx_ref, vec_ref, dwc_ref, dwe_ref, dwo_ref,
+    lo_ref, dt1_ref, g_all, vec_ref, dwc_hbm, dwe_hbm, dwo_ref,
+    we_ref, wc_ref, dwc_ref, dwe_ref, g_sc,
     wide_ref, unit_ref, sw_ref, su_ref, act_sc, gh_sc, low_sc, gb_sc, ga_sc, ctx_sc, gelu_sc, slope_sc,
+    l_w, l_o, l_g, s_g, r_g,
 ):
     i = pl.program_id(0)
     block = tok_ref.shape[0]
     units = we_ref.shape[1]
     rows = pl.ds(pl.multiple_of(i * block, block), block)
+    s, w = lax.axis_index("seq"), lax.axis_index("wt")
+    others = [flip(s, k) for k in (1, 2, 3)]
+    part_rows = g_all.shape[0]
+    weights = [
+        pltpu.make_async_copy(we_hbm, we_ref, l_w.at[0]),
+        pltpu.make_async_copy(wc_hbm, wc_ref, l_w.at[1]),
+    ]
+
+    def leaving(t):
+        there = g_all.at[:, pl.ds(pl.multiple_of((s * steps + t) * block, 128), block)]
+
+        def part(p):
+            lanes = pl.ds(pl.multiple_of(t * block, 128), block)
+            return g_sc.at[pl.ds(pl.multiple_of(p * part_rows, 16), part_rows), lanes]
+
+        copies = [
+            remote(part(p), there, (s_g, r_g), 3 * t + k, (p, w)) for k, p in enumerate(others)
+        ]
+        return copies + [pltpu.make_async_copy(part(s), there, l_g.at[t])]
 
     @pl.when(i == 0)
     def _():
+        for copy in weights:
+            copy.start()
+        meet([(p, w) for p in others])
         sw_ref[...] = jnp.zeros_like(sw_ref)
         su_ref[...] = jnp.zeros_like(su_ref)
 
@@ -990,6 +981,12 @@
     low = first.astype(bf16)
     low_sc[rows, :] = low
     branch = first + wide(CON_BIAS)
+
+    @pl.when(i == 0)
+    def _():
+        for copy in weights:
+            copy.wait()
+
     for j in range(units // chunk):
         cols = slice(j * chunk, (j + 1) * chunk)
         hidden = mm(low, we_ref[:, cols]) + unit_ref[0:1, cols]
@@ -1030,7 +1027,9 @@
     ga = dt1.astype(bf16)
     ga_sc[rows, :] = ga
     add_sum(sw_ref, S_OUT_BIAS, full, ga.astype(f32))
-    gctx_ref[...] = mm(wo_ref[...], ga, NT).astype(bf16)
+    g_sc[:, rows] = mm(wo_ref[...], ga, NT).astype(bf16)
+    for copy in leaving(i):
+        copy.start()
 
     @pl.when(i == steps - 1)
     def _():
@@ -1042,7 +1041,16 @@
             part = mm(low_sc[...], gh_sc[:, cols], TN).astype(bf16)
             for k in range(2 * dwe_ref.shape[2]):
                 dwe_ref[k % 2, j, k // 2] = part[k * own : (k + 1) * own]
+            for copy in given(j):
+                copy.start()
             return carry
+
+        def given(j):
+            there = pl.ds(pl.multiple_of(j * wide_cols, 128), wide_cols)
+            return [
+                pltpu.make_async_copy(dwc_ref.at[there], dwc_hbm.at[there], l_o.at[j]),
+                pltpu.make_async_copy(dwe_ref.at[:, j], dwe_hbm.at[:, j], l_o.at[4 + j]),
+            ]
 
         lax.fori_loop(0, 4, weight_grads, 0)
         own, part_cols = dwo_ref.shape[3:]
@@ -1057,6 +1065,12 @@
         for k in range(vec_ref.shape[0]):
             vec_ref[k, 0:8, 0:own_wide] = sw_ref[:, k * own_wide : (k + 1) * own_wide]
             vec_ref[k, 8:16, :] = su_ref[:, k * own_units : (k + 1) * own_units]
+        for t in range(steps):
+            for copy in leaving(t):
+                copy.wait()
+        for j in range(4):
+            for copy in given(j):
+                copy.wait()
 
 
 def feed_forward(n, kept, ctx_t, tokens, cotangent, wo, we, wc, *vectors):
@@ -1083,7 +1097,7 @@
         out_shape=(
             jax.ShapeDtypeStruct((rows, d), bf16),
             jax.ShapeDtypeStruct((rows, d), f32),
-            jax.ShapeDtypeStruct((d, rows), bf16),
+            jax.ShapeDtypeStruct((d // 4, 4 * rows), bf16),
             jax.ShapeDtypeStruct((n, 16, units // n), f32),
             jax.ShapeDtypeStruct((units, d), bf16),
             jax.ShapeDtypeStruct(halves, bf16),
@@ -1092,14 +1106,19 @@
         grid=(steps,),
         in_specs=[
             pl.BlockSpec(memory_space=pltpu.SMEM),
-            lanes, tile, tile, once((d, d)), once((d, units)), once((units, d)),
+            lanes, tile, tile, once((d, d)), ANYWHERE, ANYWHERE,
         ]
         + [IN_VMEM] * len(vectors),
         out_specs=(
-            tile, tile, lanes, once3((n, 16, units // n)), once((units, d)),
-            once5(halves), once5(out_halves),
+            tile, tile, ANYWHERE, once3((n, 16, units // n)), ANYWHERE,
+            ANYWHERE, once5(out_halves),
         ),
         scratch_shapes=[
+            pltpu.VMEM((d, units), bf16),
+            pltpu.VMEM((units, d), bf16),
+            pltpu.VMEM((units, d), bf16),
+            pltpu.VMEM(halves, bf16),
+            pltpu.VMEM((d, rows), bf16),
             pltpu.VMEM((8, d), f32),
             pltpu.VMEM((8, units), f32),
             pltpu.VMEM((8, d), f32),
@@ -1112,8 +1131,14 @@
             pltpu.VMEM((d, rows), bf16),
             pltpu.VMEM((block, units), keep),
             pltpu.VMEM((block, units), keep),
-        ],
-        compiler_params=pltpu.CompilerParams(vmem_limit_bytes=60 * 2**20),
+            pltpu.SemaphoreType.DMA((2,)),
+            pltpu.SemaphoreType.DMA((8,)),
+            pltpu.SemaphoreType.DMA((steps,)),
+        ]
+        + dma_sems(3 * steps),
+        compiler_params=pltpu.CompilerParams(
+            collective_id=4, has_side_effects=True, vmem_limit_bytes=62 * 2**20
+        ),
         cost_estimate=pl.CostEstimate(
             flops=rows * d * (12 * units + 6 * d),
             bytes_accessed=4 * d * (4 * units + 2 * d) + 12 * rows * d,

time: 293 us -> 288 us (0.983)
  Pallas kernels: 277 us -> 270 us
    pallas_call x1, Pallas kernels: 90.8 us -> 84.6 us  [attend_back(): pl.pallas_call(functools.partial(attend_back_kernel, heads, n), out_shape...]
  transfers between devices with their start and end apart: 4 -> 4, of which waited for: 0 -> 0; matrix products, arithmetic and copies ran while one was open for 0% -> 0% of each run, Pallas kernels for 80% -> 79%
where the time goes in v1:
time: 288 us; the launch traced here: 287 us
  Pallas kernels  270 us (94%)
  between operations  13.9 us (5%)
    pallas_call x1, Pallas kernels, attend_back(): pl.pallas_call(functools.partial(attend_back_kernel, heads, n), out_shape...  84.6 us
    pallas_call x1, Pallas kernels, attend(): pl.pallas_call(functools.partial(attend_kernel, heads, n), out_shape=(jax...  50.9 us
    pallas_call x1, Pallas kernels, gather_in(): pl.pallas_call(functools.partial(gather_kernel, n), out_shape=(jax.ShapeD...  46.7 us
    pallas_call x1, Pallas kernels, feed_forward(): pl.pallas_call(functools.partial(feed_forward_kernel, steps, chunk), out_...  45.3 us
    pallas_call x1, Pallas kernels, final(): pl.pallas_call(functools.partial(final_kernel, heads, n), out_shape=(jax....  36.4 us
    pallas_call x1, Pallas kernels, finish(): pl.pallas_call(functools.partial(finish_kernel, n, heads), out_shape=(jax...  6.16 us
  transfers between devices with their start and end apart: 4, of which 0 were waited for; matrix products, arithmetic and copies ran while one was open for 0% of the time, Pallas kernels for 79%

profile of v1, /device:TPU:0, one launch (start us, length us, event | category | flops | bytes accessed | tf_op | source)
XLA Modules:
  0.0 287.2 jit_solution(1635421158390332701)
XLA Ops:
  7.2 0.0 copy-start.1
  7.2 0.0 all-gather.4.cloned.1.call-start
  7.2 0.7 all-gather.4.cloned.1.call-update
  7.9 0.0 all-gather.6.cloned.1.call-start
  8.0 46.7 %gather_in.1 = (bf16[3072,768]{1,0:T(8,128)(2,1)}, bf16[8,96,576]{2,1,0:T(8,128)(2,1)}, bf16[4,96,768]{2,1,0:T(8,128)(2,1)}) custom-call(bf16[768,768]{1,0:T(8,128)(2,1)} %tok_ref.3, bf16[96,2304]{1,0:T(8,128)(2,1)} %weight_ref.1, bf16[96,3072]{1,0:T(8,128)(2,1)} %exp_ref.1), custom_call_target="tpu_custom_call" | custom-call | tf_op jit(solution)/shard_map/gather_in/pallas_call | solution.py:645
  54.7 0.0 all-gather.6.cloned.1.call-update
  54.7 0.0 all-gather.8.cloned.1.call-start
  54.8 0.7 all-gather.8.cloned.1.call-update
  55.5 0.0 reduce-scatter.2.cloned.1.call-start
  55.5 0.0 copy-done.1
  55.5 0.7 copy.42.lens_ref
  56.2 50.9 %attend.1 = (bf16[3,3072,192]{2,1,0:T(8,128)(2,1)}, bf16[192,3072]{1,0:T(8,128)(2,1)}, f32[3,1,3072]{2,1,0:T(1,128)}, bf16[768,768]{1,0:T(8,128)(2,1)}, bf16[4,2,96,3072]{3,2,1,0:T(8,128)(2,1)}) custom-call(s32[8,2]{1,0:T(8,128)} %copy.42.lens_ref, s32[8]{0:T(128)} %kept_ref.5, f32[12]{0:T(128)} %gate_ref.5, s32[12]{0:T(128)} %mask_ref.5, ...), custom_call_target="tpu_custom_call" | custom-call | flops 20434649088 | bytes 8257536 | tf_op jit(solution)/shard_map/attend/pallas_call | solution.py:215
  107.1 0.0 all-gather.4.cloned.1.call-done.wo_ref
  107.1 0.0 all-gather.6.cloned.1.call-done.wc_hbm
  107.1 45.3 %feed_forward.1 = (bf16[768,768]{1,0:T(8,128)(2,1)}, f32[768,768]{1,0:T(8,128)}, bf16[192,3072]{1,0:T(8,128)(2,1)}, f32[8,16,384]{2,1,0:T(8,128)}, bf16[3072,768...) custom-call(s32[8]{0:T(128)} %kept_ref.4, ...), custom_call_target="tpu_custom_call" | custom-call | flops 24461180928 | bytes 49545216 | tf_op jit(solution)/shard_map/feed_forward/pallas_call | solution.py:1095
  152.4 0.0 reduce-scatter.2.cloned.1.call-update
  152.5 84.6 %attend_back.1 = (bf16[3,4,192,768]{3,2,1,0:T(8,128)(2,1)}, bf16[8,96,576]{2,1,0:T(8,128)(2,1)}, bf16[96,768]{1,0:T(8,128)(2,1)}, bf16[96,192]{1,0:T(8,128)(2,1)}, f32[8,192]{1,0:T(8,128)}) custom-call(s32[8,2]{1,0:T(8,128)} %copy.42.lens_ref, s32[8]{0:T(128)} %kept_ref.5, f32[12]{0:T(128)} %gate_ref.5, s32[12]{0:T(128)} %mask_ref.5, ...), custom_call_target="tpu_custom_call" | custom-call | flops 47009759232 | bytes 15335424 | tf_op jit(solution)/shard_map/attend_back/pallas_call | solution.py:491
  237.1 0.0 all-gather.8.cloned.1.call-done.w_hbm
  237.1 0.0 reduce-scatter.2.cloned.1.call-done
  237.1 36.4 %final.1 = (f32[768,768]{1,0:T(8,128)}, bf16[4,96,768]{2,1,0:T(8,128)(2,1)}, bf16[4,96,192]{2,1,0:T(8,128)(2,1)}, bf16[4,96,768]{2,1,0:T(8,128)(2,1)}, bf16[4,96...) custom-call(f32[768,768]{1,0:T(8,128)} %get-tuple-element.72.base_hbm, ...), custom_call_target="tpu_custom_call" | custom-call | flops 2717908992 | bytes 3538944 | tf_op jit(solution)/shard_map/final/pallas_call | solution.py:776
  273.5 0.0 copy-start
  273.5 6.2 %finish.1 = (f32[4,96,768]{2,1,0:T(8,128)}, f32[96,768]{1,0:T(8,128)}, f32[96,3072]{1,0:T(8,128)}, f32[96,2304]{1,0:T(8,128)}, f32[768,768]{1,0:T(8,128)}, /*ind...) custom-call(f32[12]{0:T(128)} %gate_ref.5, ...), custom_call_target="tpu_custom_call" | custom-call | tf_op jit(solution)/shard_map/finish/pallas_call | solution.py:863
  279.7 0.0 copy-done
  279.7 1.0 copy.45
Async XLA Ops:
  7.2 48.3 %copy-start.1 = (s32[8,2]{0,1:T(2,128)S(1)}, s32[8,2]{0,1:T(2,128)}, u32[]{:S(2)}) copy-start(s32[8,2]{0,1:T(2,128)} %param.47) | copy-start | bytes 196
  7.2 99.9 %all-gather.4.cloned.1.call-start = ((), (), s32[]{:S(2)}) async-start(), calls=%async_computation.1 | async-start | bytes 1327104 | tf_op jit(solution)/shard_map/all_gather | solution.py:1186
  7.9 99.2 %all-gather.6.cloned.1.call-start = ((), (), s32[]{:S(2)}) async-start(), calls=%async_computation.2 | async-start | bytes 5308416 | tf_op jit(solution)/shard_map/all_gather | solution.py:1184
  54.7 182.3 %all-gather.8.cloned.1.call-start = ((), (), s32[]{:S(2)}) async-start(), calls=%async_computation.3 | async-start | bytes 3981312 | tf_op jit(solution)/shard_map/all_gather | solution.py:1185
  55.5 181.6 %reduce-scatter.2.cloned.1.call-start = ((), (), s32[]{:S(2)}) async-start(), calls=%async_computation.4 | async-start | bytes 5308416 | tf_op jit(solution)/shard_map/reduce_scatter | solution.py:1229
  273.5 6.2 %copy-start = (bf16[768,768]{1,0:T(8,128)(2,1)S(1)}, bf16[768,768]{1,0:T(8,128)(2,1)}, u32[]{:S(2)}) copy-start(bf16[768,768]{1,0:T(8,128)(2,1)} %get-tuple-element.128) | copy-start | bytes 3538948
Sparse Core Ops, SparseCore 0:
  9.7 35.7 all-gather.3
  54.8 49.8 all-gather.5
  106.4 40.3 all-gather.7
  152.6 55.2 reduce-scatter.1

commit v2 on v1

--- a/solution.py
+++ b/solution.py
@@ -80,8 +80,8 @@
 
 def attend_kernel(
     heads, n, lens_ref, kept_ref, gate_ref, mask_ref, qb_ref, vb_ref, tok_ref, w_ref, exp_ref,
-    packed_ref, ctx_ref, lse_ref, full_ref, exp_all,
-    q_sc, k_sc, vt_sc, ct_sc, vec_ref, exp_buf,
+    q_sc, k_sc, v_ref, kt_ref, ctx_ref, lse_ref, full_ref, exp_all,
+    vt_sc, ct_sc, vec_ref, exp_buf,
     local_sem, s_sem, r_sem, s_e, r_e,
 ):
     s, w = lax.axis_index("seq"), lax.axis_index("wt")
@@ -129,10 +129,13 @@
         x = (x * vec_ref[1:2, :]).astype(bf16)
         for h in range(heads):
             at = 3 * HD * h
-            packed_ref[h, rows, :] = x[:, at : at + 3 * HD]
             q_sc[h, rows, :] = x[:, at : at + HD]
-            k_sc[h, rows, :] = x[:, at + HD : at + 2 * HD]
-            vt_sc[h, :, rows] = x[:, at + 2 * HD : at + 3 * HD].T
+            k = x[:, at + HD : at + 2 * HD]
+            k_sc[h, rows, :] = k
+            kt_ref[h, i] = k.T
+            v = x[:, at + 2 * HD : at + 3 * HD]
+            v_ref[h, rows, :] = v
+            vt_sc[h, :, rows] = v.T
         return carry
 
     lax.fori_loop(0, GLEN // TQ, project, 0)
@@ -215,17 +218,18 @@
     return pl.pallas_call(
         functools.partial(attend_kernel, heads, n),
         out_shape=(
-            jax.ShapeDtypeStruct((heads, GLEN, 3 * HD), bf16),
+            jax.ShapeDtypeStruct((heads, GLEN, HD), bf16),
+            jax.ShapeDtypeStruct((heads, GLEN, HD), bf16),
+            jax.ShapeDtypeStruct((heads, GLEN, HD), bf16),
+            jax.ShapeDtypeStruct((heads, GLEN // TQ, HD, TQ), bf16),
             jax.ShapeDtypeStruct((HD * heads, GLEN), bf16),
             jax.ShapeDtypeStruct((heads, 1, GLEN), f32),
             jax.ShapeDtypeStruct((4 * HD * heads, GLEN // 4), bf16),
             jax.ShapeDtypeStruct((n // 2, 2, exp_part.shape[1], 4 * exp_part.shape[2]), bf16),
         ),
         in_specs=[IN_SMEM] * 4 + [IN_VMEM] * 4 + [ANYWHERE],
-        out_specs=(IN_VMEM, IN_VMEM, IN_VMEM, ANYWHERE, ANYWHERE),
+        out_specs=(IN_VMEM,) * 6 + (ANYWHERE, ANYWHERE),
         scratch_shapes=[
-            pltpu.VMEM((heads, GLEN, HD), bf16),
-            pltpu.VMEM((heads, GLEN, HD), bf16),
             pltpu.VMEM((heads, HD, GLEN), bf16),
             pltpu.VMEM((GLEN // TQ, HD, TQ), bf16),
             pltpu.VMEM((2, width), f32),
@@ -248,30 +252,41 @@
 
 
 def attend_back_kernel(
-    heads, n, lens_ref, kept_ref, gate_ref, mask_ref, packed_hbm, ctx_ref, gctx_ref, lse_ref, tok_hbm,
-    e_hbm, o_hbm, pieces_o, dw_o, exp_o, out_o, late_o,
-    packed_v, tok_v, e_own, o_own, e_got, o_got, e_all, o_all, e_sum, o_sum, e_z, o_z, stage, late_sc,
-    q_sc, k_sc, v_sc, kt_sc, g_sc, g_nat, delta_sc, delta_nat, dqt_sc, dk_sc, dv_sc, acc,
-    l_in, l_out, s_p, r_p, s_c, r_c, s_e, r_e, s_z, r_z,
+    heads, n, lens_ref, kept_ref, gate_ref, mask_ref, q_hbm, k_hbm, v_hbm, kt_hbm,
+    ctx_ref, gctx_ref, lse_ref, tok_hbm,
+    e_own_hbm, e_got_hbm, o_own_hbm, o_got_hbm, pieces_o, dw_o, exp_o, out_o, late_o,
+    tok_v, e_own, o_own, e_got, o_got, e_all, o_all, e_sum, o_sum, e_z, o_z, stage, late_sc, row_sc,
+    q_all, k_all, v_all, kt_all, g_sc, g_nat, delta_sc, delta_nat, dqt_sc, dk_sc, dv_sc, acc,
+    l_in, l_out, s_p, r_p, s_e, r_e, s_z, r_z,
 ):
     s, w = lax.axis_index("seq"), lax.axis_index("wt")
     others = [flip(s, k) for k in (1, 2, 3)]
-    mate = (s, flip(w, 1))
     z, c, nz = w // 2, lax.rem(w, 2), n // 2
     far = [lax.rem(z + j, nz) for j in range(1, nz)]
     short_first = lens_ref[w, 0] == SHORT
     count = GLEN // 4
     width = heads * HD
+    def taken(h):
+        pairs = ((q_hbm, q_all), (k_hbm, k_all), (v_hbm, v_all), (kt_hbm, kt_all))
+        return [
+            pltpu.make_async_copy(src.at[h], dst.at[h], l_in.at[4 * h + k])
+            for k, (src, dst) in enumerate(pairs)
+        ]
+
     loads = [
-        pltpu.make_async_copy(packed_hbm.at[h], packed_v.at[h], l_in.at[h]) for h in range(heads)
-    ] + [
-        pltpu.make_async_copy(e_hbm.at[c], e_own, l_in.at[heads]),
-        pltpu.make_async_copy(o_hbm.at[c], o_own, l_in.at[heads + 1]),
-        pltpu.make_async_copy(tok_hbm, tok_v, l_in.at[heads + 2]),
+        pltpu.make_async_copy(e_own_hbm, e_own, l_in.at[4 * heads]),
+        pltpu.make_async_copy(e_got_hbm, e_got, l_in.at[4 * heads + 1]),
+        pltpu.make_async_copy(o_own_hbm, o_own, l_in.at[4 * heads + 2]),
+        pltpu.make_async_copy(o_got_hbm, o_got, l_in.at[4 * heads + 3]),
+        pltpu.make_async_copy(tok_hbm, tok_v, l_in.at[4 * heads + 4]),
     ]
-    for copy in loads:
+    for copy in loads[:4] + taken(0):
         copy.start()
-    meet([(p, w) for p in others] + [mate] + [(s, 2 * k + c) for k in far])
+    for h in range(1, heads):
+        for copy in taken(h):
+            copy.start()
+    loads[4].start()
+    meet([(p, w) for p in others] + [(s, 2 * k + c) for k in far])
 
     def leaving(h, own=False):
         if own:
@@ -281,10 +296,6 @@
             for k, p in enumerate(others)
         ]
 
-    over_pair = [
-        remote(e_hbm.at[1 - c], e_got, (s_c, r_c), 0, mate),
-        remote(o_hbm.at[1 - c], o_got, (s_c, r_c), 1, mate),
-    ]
     over_plane = [
         remote(e_got.at[p], e_all.at[s], (s_e, r_e), k, (p, w)) for k, p in enumerate(others)
     ] + [remote(o_got.at[p], o_all.at[s], (s_e, r_e), 3 + k, (p, w)) for k, p in enumerate(others)]
@@ -294,24 +305,27 @@
         remote(o_sum.at[k], o_z.at[z], (s_z, r_z), nz - 1 + j, (s, 2 * k + c))
         for j, k in enumerate(far)
     ]
-    for copy in over_pair:
+    for copy in loads[:4]:
+        copy.wait()
+
+    def pair_sum(i, carry):
+        q, k = i // nz, lax.rem(i, nz)
+        e_got[q, k] = (e_got[q, k].astype(f32) + e_own[q, k].astype(f32)).astype(bf16)
+        o_got[q, k] = (o_got[q, k].astype(f32) + o_own[q, k].astype(f32)).astype(bf16)
+        return carry
+
+    lax.fori_loop(0, 4 * nz, pair_sum, 0)
+    for copy in over_plane:
         copy.start()
+    e_all[s] = e_got[s]
+    o_all[s] = o_got[s]
     late_sc[...] = jnp.zeros_like(late_sc)
+    row_sc[...] = jnp.zeros_like(row_sc)
+    for h in range(heads):
+        for copy in taken(h):
+            copy.wait()
 
     def prologue(h):
-        pltpu.make_async_copy(packed_hbm.at[h], packed_v.at[h], l_in.at[h]).wait()
-
-        def split(i, carry):
-            rows = pl.ds(pl.multiple_of(i * TQ, TQ), TQ)
-            x = packed_v[h, rows, :]
-            q_sc[i] = x[:, 0:HD]
-            k = x[:, HD : 2 * HD]
-            k_sc[i] = k
-            kt_sc[i] = k.T
-            v_sc[i] = x[:, 2 * HD : 3 * HD]
-            return carry
-
-        lax.fori_loop(0, GLEN // TQ, split, 0)
         dk_sc[...] = jnp.zeros_like(dk_sc)
         dv_sc[...] = jnp.zeros_like(dv_sc)
         def inner(i, carry):
@@ -330,42 +344,24 @@
         lax.fori_loop(0, GLEN // TQ, inner, 0)
         lax.fori_loop(0, GLEN // TQ, order, 0)
 
-    def halfway(h):
-        if h == 0:
-            loads[heads].wait()
-            loads[heads + 1].wait()
-            for copy in over_pair:
-                copy.wait_recv()
-
-            def pair_sum(i, carry):
-                q, k = i // nz, lax.rem(i, nz)
-                e_got[q, k] = (e_got[q, k].astype(f32) + e_own[q, k].astype(f32)).astype(bf16)
-                o_got[q, k] = (o_got[q, k].astype(f32) + o_own[q, k].astype(f32)).astype(bf16)
-                return carry
-
-            lax.fori_loop(0, 4 * nz, pair_sum, 0)
-            for copy in over_plane:
-                copy.start()
-            e_all[s] = e_got[s]
-            o_all[s] = o_got[s]
-        if h == heads - 1:
-            for copy in over_plane:
-                copy.wait_recv()
-
-            def add4(ref, k):
-                t = [ref[q, k].astype(f32) for q in range(4)]
-                return ((t[0] + t[1]) + (t[2] + t[3])).astype(bf16)
-
-            def plane_sum(k, carry):
-                e_sum[k] = add4(e_all, k)
-                o_sum[k] = add4(o_all, k)
-                return carry
-
-            lax.fori_loop(0, nz, plane_sum, 0)
-            for copy in over_z:
-                copy.start()
-            e_z[z] = e_sum[z]
-            o_z[z] = o_sum[z]
+    def halfway():
+        for copy in over_plane:
+            copy.wait_recv()
+
+        def add4(ref, k):
+            t = [ref[q, k].astype(f32) for q in range(4)]
+            return ((t[0] + t[1]) + (t[2] + t[3])).astype(bf16)
+
+        def plane_sum(k, carry):
+            e_sum[k] = add4(e_all, k)
+            o_sum[k] = add4(o_all, k)
+            return carry
+
+        lax.fori_loop(0, nz, plane_sum, 0)
+        for copy in over_z:
+            copy.start()
+        e_z[z] = e_sum[z]
+        o_z[z] = o_sum[z]
 
     def epilogue(h, first, last):
         half = SHORT // 2
@@ -374,13 +370,15 @@
         def settle(j, carry):
             i = ordered_at(short_first, j)
             dq = dqt_sc[i].astype(bf16)
-            dk = (dk_sc[i] * score_scale).T.astype(bf16)
-            dv = dv_sc[i].T.astype(bf16).astype(f32)
-            gate = dv * v_sc[i].T.astype(f32)
+            dk = (dk_sc[i] * score_scale).astype(bf16).T
+            dv = dv_sc[i].astype(bf16).astype(f32)
+            gate = jnp.sum(dv * v_all[h, i].astype(f32), axis=0, keepdims=True)
             dv = (dv * scale).astype(bf16)
-            for row, x in ((0, dq.astype(f32)), (HD, dv.astype(f32)), (2 * HD, gate)):
-                x = (x[:, 0:128] + x[:, 128:256]) + (x[:, 256:384] + x[:, 384:512])
-                late_sc[h, row : row + HD, :] += x
+            row_sc[h, 0:1, :] += jnp.sum(dv.astype(f32), axis=0, keepdims=True)
+            row_sc[h, 1:2, :] += gate
+            dv = dv.T
+            x = dq.astype(f32)
+            late_sc[h] += (x[:, 0:128] + x[:, 128:256]) + (x[:, 256:384] + x[:, 384:512])
             for r in range(2):
                 u = 2 * j + r
                 p, there = u // 3, pl.ds(pl.multiple_of(lax.rem(u, 3) * half, half), half)
@@ -402,19 +400,19 @@
 
     def tile_of(h):
         def tile(i, own_blocks):
-            q = q_sc[i]
+            q = q_all[h, i]
             g = g_sc[i]
             lse = lse_ref[h, :, pl.ds(pl.multiple_of(i * TQ, TQ), TQ)]
             delta = delta_sc[i]
             dq = jnp.zeros((HD, TQ), f32)
             for j in (0, 1) + own_blocks:
-                sc = mm(k_sc[j], q, NT)
+                sc = mm(k_all[h, j], q, NT)
                 p = jnp.exp2(sc * exp2_scale - lse)
-                dp = mm(v_sc[j], g)
+                dp = mm(v_all[h, j], g)
                 ds = (p * (dp - delta)).astype(bf16)
                 dv_sc[j] += mm(p.astype(bf16), g, NT)
                 dk_sc[j] += mm(ds, q)
-                dq = dq + mm(kt_sc[j], ds)
+                dq = dq + mm(kt_all[h, j], ds)
             dqt_sc[i] = dq * score_scale
 
         return tile
@@ -430,11 +428,7 @@
             return carry
 
         tile_of(h)(2, (2,))
-        for j in (0, heads - 1):
-
-            @pl.when(h == j)
-            def _(j=j):
-                halfway(j)
+        pl.when(h == heads - 1)(halfway)
 
         lax.fori_loop(3, 6, longer, 0)
         epilogue(h, 2, 6)
@@ -443,7 +437,7 @@
         return carry
 
     lax.fori_loop(0, heads, one_head, 0)
-    loads[heads + 2].wait()
+    loads[4].wait()
     acc[...] = jnp.zeros_like(acc)
 
     def weight_grad(p, carry):
@@ -459,9 +453,9 @@
         dw_o[k] = grad[k * own_rows : (k + 1) * own_rows, :]
     late_o[...] = jnp.zeros_like(late_o)
     for h in range(heads):
-        sums = jnp.sum(late_sc[h].T, axis=0, keepdims=True)
-        for k in range(3):
-            late_o[k : k + 1, HD * h : HD * (h + 1)] = sums[:, HD * k : HD * (k + 1)]
+        own = slice(HD * h, HD * (h + 1))
+        late_o[0:1, own] = jnp.sum(late_sc[h].T, axis=0, keepdims=True)
+        late_o[1:3, own] = row_sc[h, 0:2, :]
     for copy in over_z:
         copy.wait_recv()
     for ref, out in ((e_z, exp_o), (o_z, out_o)):
@@ -472,22 +466,22 @@
     for h in range(heads):
         for copy in [leaving(h, True)] + leaving(h):
             copy.wait()
-    for copy in over_pair + over_plane + over_z:
+    for copy in over_plane + over_z:
         copy.wait_send()
 
 
-def attend_back(n, lens, kept, gate, mask, packed, ctx, g, lse, tokens_all, e_parts, o_parts):
-    heads = packed.shape[0]
+def attend_back(n, lens, kept, gate, mask, q, k, v, kt, ctx, g, lse, tokens_all, *parts):
+    heads = q.shape[0]
     width = 3 * HD * heads
     d = tokens_all.shape[1]
     count = GLEN // 4
     nz = n // 2
-    own, wide = e_parts.shape[3:]
-    part = o_parts.shape[4]
+    own, wide = parts[0].shape[2:]
+    part = parts[2].shape[3]
     blocks = GLEN // TQ
-    rows64 = pltpu.VMEM((blocks, TQ, HD), bf16)
+    rows64 = pltpu.VMEM((heads, blocks, TQ, HD), bf16)
     blocks64 = pltpu.VMEM((blocks, HD, TQ), bf16)
-    quarters = [pltpu.VMEM(e_parts.shape[1:], bf16), pltpu.VMEM(o_parts.shape[1:], bf16)]
+    quarters = [pltpu.VMEM(parts[0].shape, bf16), pltpu.VMEM(parts[2].shape, bf16)]
     return pl.pallas_call(
         functools.partial(attend_back_kernel, heads, n),
         out_shape=(
@@ -498,21 +492,22 @@
             jax.ShapeDtypeStruct((8, HD * heads), f32),
         ),
         in_specs=[IN_SMEM] * 4
-        + [ANYWHERE, IN_VMEM, IN_VMEM, IN_VMEM, ANYWHERE]
-        + [ANYWHERE] * 2,
+        + [ANYWHERE] * 4
+        + [IN_VMEM, IN_VMEM, IN_VMEM, ANYWHERE]
+        + [ANYWHERE] * 4,
         out_specs=(ANYWHERE, IN_VMEM, IN_VMEM, IN_VMEM, IN_VMEM),
         scratch_shapes=[
-            pltpu.VMEM(packed.shape, bf16),
             pltpu.VMEM(tokens_all.shape, bf16),
         ]
         + quarters * 3
         + [pltpu.VMEM((nz, own, wide), bf16), pltpu.VMEM((nz, own, part), bf16)] * 2
-        + [pltpu.VMEM((heads, 4, 3 * HD, count), bf16), pltpu.VMEM((heads, 3 * HD, 128), f32)]
+        + [pltpu.VMEM((heads, 4, 3 * HD, count), bf16), pltpu.VMEM((heads, HD, 128), f32)]
+        + [pltpu.VMEM((heads, 8, HD), f32)]
         + [
             rows64,
             rows64,
             rows64,
-            blocks64,
+            pltpu.VMEM(kt.shape, bf16),
             blocks64,
             blocks64,
             pltpu.VMEM((blocks, 1, TQ), f32),
@@ -521,11 +516,10 @@
             pltpu.VMEM((blocks, TQ, HD), f32),
             pltpu.VMEM((blocks, TQ, HD), f32),
             pltpu.VMEM((width, d), f32),
-            pltpu.SemaphoreType.DMA((heads + 3,)),
+            pltpu.SemaphoreType.DMA((4 * heads + 5,)),
             pltpu.SemaphoreType.DMA((heads,)),
         ]
         + dma_sems(3 * heads)
-        + dma_sems(2)
         + dma_sems(6)
         + dma_sems(2 * nz - 2),
         compiler_params=remote_params(2),
@@ -535,7 +529,11 @@
             transcendentals=heads * 5767168,
         ),
         name="attend_back",
-    )(lens, kept, gate, mask, packed, ctx, g, lse, tokens_all, e_parts, o_parts)
+    )(
+        lens, kept, gate, mask,
+        *(x.reshape(heads, blocks, TQ, HD) for x in (q, k, v)),
+        kt, ctx, g, lse, tokens_all, *parts,
+    )
 
 
 def meet(peers):
@@ -808,29 +806,41 @@
 
 
 def finish_kernel(n, heads, gate_ref, mask_ref, *refs):
-    sources, rest = refs[:7], refs[7:]
-    con_o, out_o, exp_o, att_o, tok_o = rest[:5]
-    vec_os, unit_os, query_o, value_o, gate_o = rest[5:12], rest[12:14], rest[14], rest[15], rest[16]
-    con_v, out_v, exp_v, att_v, vec_v, late_v, sem = rest[17:]
+    sources, rest = refs[:8], refs[8:]
+    con_o, exp_o, att_o, tok_o, low_o, out_o = rest[:6]
+    vec_os, unit_os, query_o, value_o, gate_o = rest[6:13], rest[13:15], rest[15], rest[16], rest[17]
+    con_v, exp_v, att_v, tok_v, low_v, out_v, vec_v, late_v, con_f, exp_f, att_f, l_in, l_out = rest[18:]
+    inside = (con_v, exp_v, att_v, tok_v, low_v, out_v, vec_v, late_v)
     loads = [
-        pltpu.make_async_copy(src, dst, sem.at[k])
-        for k, (src, dst) in enumerate(
-            zip(sources, (con_v, out_v, exp_v, att_v, vec_v, late_v, tok_o), strict=True)
-        )
+        pltpu.make_async_copy(src, dst, l_in.at[k])
+        for k, (src, dst) in enumerate(zip(sources, inside, strict=True))
     ]
     for copy in loads:
         copy.start()
+    outside = ((con_f, con_o), (exp_f, exp_o), (att_f, att_o), (tok_v, tok_o), (low_v, low_o))
+    stores = [pltpu.make_async_copy(src, dst, l_out.at[k]) for k, (src, dst) in enumerate(outside)]
 
     def add4(parts):
         return (parts[0] + parts[1]) + (parts[2] + parts[3])
 
-    for copy in loads:
+    wide, cols, part = exp_v.shape[2], att_v.shape[2], out_v.shape[2]
+    loads[0].wait()
+    con_f[...] = con_v[...].astype(f32)
+    stores[0].start()
+    loads[1].wait()
+    for k in range(4):
+        exp_f[:, k * wide : (k + 1) * wide] = exp_v[k].astype(f32)
+    stores[1].start()
+    loads[2].wait()
+    for k in range(4):
+        att_f[:, k * cols : (k + 1) * cols] = att_v[k].astype(f32)
+    stores[2].start()
+    for k in (3, 4):
+        loads[k].wait()
+        stores[k].start()
+    for copy in loads[5:]:
         copy.wait()
-    wide, cols, part = exp_v.shape[2], att_v.shape[2], out_v.shape[2]
     for k in range(4):
-        con_o[k] = con_v[k].astype(f32)
-        exp_o[:, k * wide : (k + 1) * wide] = exp_v[k].astype(f32)
-        att_o[:, k * cols : (k + 1) * cols] = att_v[k].astype(f32)
         out_o[:, k * part : (k + 1) * part] = out_v[k].astype(f32)
     vec = add4([vec_v[k] for k in range(4)])
     own = vec_os[0].shape[0]
@@ -853,33 +863,44 @@
             kept = mask_ref[heads * k + h].astype(f32) / gate_ref[heads * k + h]
             gates.append(part_sum * kept)
     gate_o[...] = jnp.concatenate(gates, axis=1)[0]
-
-
-def finish(n, heads, gate, mask, con, out, exp_all, att, vec, late, tok):
+    for copy in stores:
+        copy.wait()
+
+
+def finish(n, heads, gate, mask, con, exp_all, att, tok, low, out, vec, late):
     r = out.shape[1]
     wide, cols, part = exp_all.shape[2], att.shape[2], out.shape[2]
     units = vec.shape[2]
     row = jax.ShapeDtypeStruct((r,), f32)
+    con_f, exp_f, att_f = (
+        con.shape,
+        (r, 4 * wide),
+        (r, 4 * cols),
+    )
     return pl.pallas_call(
         functools.partial(finish_kernel, n, heads),
         out_shape=(
-            jax.ShapeDtypeStruct(con.shape, f32),
+            jax.ShapeDtypeStruct(con_f, f32),
+            jax.ShapeDtypeStruct(exp_f, f32),
+            jax.ShapeDtypeStruct(att_f, f32),
+            jax.ShapeDtypeStruct(tok.shape, f32),
+            jax.ShapeDtypeStruct(low.shape, low.dtype),
             jax.ShapeDtypeStruct((r, 4 * part), f32),
-            jax.ShapeDtypeStruct((r, 4 * wide), f32),
-            jax.ShapeDtypeStruct((r, 4 * cols), f32),
-            jax.ShapeDtypeStruct(tok.shape, f32),
         )
         + (row,) * 7
         + (jax.ShapeDtypeStruct((units,), f32),) * 2
         + (row,) * 2
         + (jax.ShapeDtypeStruct((4 * heads,), f32),),
-        in_specs=[IN_SMEM] * 2 + [ANYWHERE] * 7,
-        out_specs=(IN_VMEM,) * 17,
-        scratch_shapes=[pltpu.VMEM(x.shape, x.dtype) for x in (con, out, exp_all, att, vec, late)]
-        + [pltpu.SemaphoreType.DMA((7,))],
+        in_specs=[IN_SMEM] * 2 + [ANYWHERE] * 8,
+        out_specs=(ANYWHERE,) * 5 + (IN_VMEM,) * 13,
+        scratch_shapes=[
+            pltpu.VMEM(x.shape, x.dtype) for x in (con, exp_all, att, tok, low, out, vec, late)
+        ]
+        + [pltpu.VMEM(x, f32) for x in (con_f, exp_f, att_f)]
+        + [pltpu.SemaphoreType.DMA((8,)), pltpu.SemaphoreType.DMA((5,))],
         compiler_params=pltpu.CompilerParams(vmem_limit_bytes=56 * 2**20),
         name="finish",
-    )(gate, mask, con, out, exp_all, att, vec, late, tok)
+    )(gate, mask, con, exp_all, att, tok, low, out, vec, late)
 
 
 (OUT_BIAS, GAIN1, SHIFT1, HIDDEN_SCALE, CON_BIAS, GAIN2, SHIFT2, HIDDEN_MASK) = range(8)
@@ -915,10 +936,10 @@
     steps, chunk,
     kept_ref, ctx_ref, tok_ref, cot_ref, wo_ref, we_hbm, wc_hbm,
     ob_ref, g1_ref, t1_ref, hg_ref, hm_ref, cb_ref, g2_ref, t2_ref, eb_ref, ug_ref, um_ref,
-    lo_ref, dt1_ref, g_all, vec_ref, dwc_hbm, dwe_hbm, dwo_ref,
-    we_ref, wc_ref, dwc_ref, dwe_ref, g_sc,
+    lo_ref, dt1_ref, g_all, vec_ref, dwc_hbm, e_own, e_got, o_own, o_got,
+    we_ref, wc_ref, dwc_ref, dwe_ref, dwo_ref, g_sc,
     wide_ref, unit_ref, sw_ref, su_ref, act_sc, gh_sc, low_sc, gb_sc, ga_sc, ctx_sc, gelu_sc, slope_sc,
-    l_w, l_o, l_g, s_g, r_g,
+    l_w, l_o, l_g, s_g, r_g, s_p, r_p,
 ):
     i = pl.program_id(0)
     block = tok_ref.shape[0]
@@ -926,6 +947,7 @@
     rows = pl.ds(pl.multiple_of(i * block, block), block)
     s, w = lax.axis_index("seq"), lax.axis_index("wt")
     others = [flip(s, k) for k in (1, 2, 3)]
+    mate, core = (s, flip(w, 1)), lax.rem(w, 2)
     part_rows = g_all.shape[0]
     weights = [
         pltpu.make_async_copy(we_hbm, we_ref, l_w.at[0]),
@@ -948,7 +970,7 @@
     def _():
         for copy in weights:
             copy.start()
-        meet([(p, w) for p in others])
+        meet([(p, w) for p in others] + [mate])
         sw_ref[...] = jnp.zeros_like(sw_ref)
         su_ref[...] = jnp.zeros_like(su_ref)
 
@@ -1049,15 +1071,22 @@
             there = pl.ds(pl.multiple_of(j * wide_cols, 128), wide_cols)
             return [
                 pltpu.make_async_copy(dwc_ref.at[there], dwc_hbm.at[there], l_o.at[j]),
-                pltpu.make_async_copy(dwe_ref.at[:, j], dwe_hbm.at[:, j], l_o.at[4 + j]),
+                pltpu.make_async_copy(dwe_ref.at[core, j], e_own.at[j], l_o.at[4 + j]),
+                remote(dwe_ref.at[1 - core, j], e_got.at[j], (s_p, r_p), j, mate),
             ]
 
-        lax.fori_loop(0, 4, weight_grads, 0)
-        own, part_cols = dwo_ref.shape[3:]
+        part_cols = dwo_ref.shape[4]
         for q in range(4):
             part = mm(ctx_sc[...], ga_sc[:, q * part_cols : (q + 1) * part_cols]).astype(bf16)
             for k in range(2 * dwo_ref.shape[2]):
                 dwo_ref[k % 2, q, k // 2] = part[k * own : (k + 1) * own]
+        over = [
+            pltpu.make_async_copy(dwo_ref.at[core], o_own, l_o.at[8]),
+            remote(dwo_ref.at[1 - core], o_got, (s_p, r_p), 4, mate),
+        ]
+        for copy in over:
+            copy.start()
+        lax.fori_loop(0, 4, weight_grads, 0)
         vec_ref[...] = jnp.zeros_like(vec_ref)
         sw_ref[S_HIDDEN : S_HIDDEN + 1, :] *= wide(HIDDEN_MASK)
         su_ref[1:2, :] *= unit_ref[2:3, :]
@@ -1068,6 +1097,8 @@
         for t in range(steps):
             for copy in leaving(t):
                 copy.wait()
+        for copy in over:
+            copy.wait()
         for j in range(4):
             for copy in given(j):
                 copy.wait()
@@ -1089,9 +1120,6 @@
     def once3(shape):
         return pl.BlockSpec(shape, lambda i: (0, 0, 0), pipeline_mode=pl.Buffered(1))
 
-    def once5(shape):
-        return pl.BlockSpec(shape, lambda i: (0, 0, 0, 0, 0), pipeline_mode=pl.Buffered(1))
-
     return pl.pallas_call(
         functools.partial(feed_forward_kernel, steps, chunk),
         out_shape=(
@@ -1100,8 +1128,10 @@
             jax.ShapeDtypeStruct((d // 4, 4 * rows), bf16),
             jax.ShapeDtypeStruct((n, 16, units // n), f32),
             jax.ShapeDtypeStruct((units, d), bf16),
-            jax.ShapeDtypeStruct(halves, bf16),
-            jax.ShapeDtypeStruct(out_halves, bf16),
+            jax.ShapeDtypeStruct(halves[1:], bf16),
+            jax.ShapeDtypeStruct(halves[1:], bf16),
+            jax.ShapeDtypeStruct(out_halves[1:], bf16),
+            jax.ShapeDtypeStruct(out_halves[1:], bf16),
         ),
         grid=(steps,),
         in_specs=[
@@ -1111,13 +1141,14 @@
         + [IN_VMEM] * len(vectors),
         out_specs=(
             tile, tile, ANYWHERE, once3((n, 16, units // n)), ANYWHERE,
-            ANYWHERE, once5(out_halves),
+            ANYWHERE, ANYWHERE, ANYWHERE, ANYWHERE,
         ),
         scratch_shapes=[
             pltpu.VMEM((d, units), bf16),
             pltpu.VMEM((units, d), bf16),
             pltpu.VMEM((units, d), bf16),
             pltpu.VMEM(halves, bf16),
+            pltpu.VMEM(out_halves, bf16),
             pltpu.VMEM((d, rows), bf16),
             pltpu.VMEM((8, d), f32),
             pltpu.VMEM((8, units), f32),
@@ -1132,10 +1163,11 @@
             pltpu.VMEM((block, units), keep),
             pltpu.VMEM((block, units), keep),
             pltpu.SemaphoreType.DMA((2,)),
-            pltpu.SemaphoreType.DMA((8,)),
+            pltpu.SemaphoreType.DMA((9,)),
             pltpu.SemaphoreType.DMA((steps,)),
         ]
-        + dma_sems(3 * steps),
+        + dma_sems(3 * steps)
+        + dma_sems(5),
         compiler_params=pltpu.CompilerParams(
             collective_id=4, has_side_effects=True, vmem_limit_bytes=62 * 2**20
         ),
@@ -1184,7 +1216,7 @@
     full_contract = lax.all_gather(contract_weight, "wt", axis=0, tiled=True)
     full_attention = lax.all_gather(attention_weight, "wt", axis=0, tiled=True)
     full_output = lax.all_gather(output_weight, "wt", axis=0, tiled=True)
-    packed, own_context, log_sums, context_t, full_expand = attend(
+    q, k, v, kt, own_context, log_sums, context_t, full_expand = attend(
         wt_count,
         continuation_lengths,
         attention_mask,
@@ -1203,8 +1235,7 @@
         grad_context_t,
         vec_sums,
         contract_weight_grad,
-        exp_parts,
-        out_parts,
+        *parts,
     ) = feed_forward(
         wt_count,
         feedforward_mask,
@@ -1233,13 +1264,15 @@
         attention_mask,
         head_gate,
         head_mask,
-        packed,
+        q,
+        k,
+        v,
+        kt,
         own_context,
         grad_context_t,
         log_sums,
         tokens_all,
-        exp_parts,
-        out_parts,
+        *parts,
     )
     tokens_grad, con_all, out_all, exp_all, att_all, vec_all, late_all = final(
         wt_count,
@@ -1253,18 +1286,19 @@
         vec_sums,
         late_sums,
     )
-    con_sum, out_sum, exp_sum, att_sum, tokens_grad, *rows = finish(
+    con_sum, exp_sum, att_sum, tokens_grad, layer_output, out_sum, *rows = finish(
         wt_count,
         local_heads,
         head_gate,
         head_mask,
         con_all,
-        out_all,
         exp_all,
         att_all,
+        tokens_grad,
+        layer_output,
+        out_all,
         vec_all,
         late_all,
-        tokens_grad,
     )
     return (
         layer_output,

time: 288 us -> 286 us (level)
  transfers between devices with their start and end apart: 4 -> 4, of which waited for: 0 -> 0; matrix products, arithmetic and copies ran while one was open for 0% -> 0% of each run, Pallas kernels for 79% -> 80%
where the time goes in v2:
time: 286 us; the launch traced here: 285 us
  Pallas kernels  269 us (94%)
  between operations  13.9 us (5%)
    pallas_call x1, Pallas kernels, attend_back(): pl.pallas_call(functools.partial(attend_back_kernel, heads, n), out_shape...  81.7 us
    pallas_call x1, Pallas kernels, attend(): pl.pallas_call(functools.partial(attend_kernel, heads, n), out_shape=(jax...  51.9 us
    pallas_call x1, Pallas kernels, feed_forward(): pl.pallas_call(functools.partial(feed_forward_kernel, steps, chunk), out_...  47 us
    pallas_call x1, Pallas kernels, gather_in(): pl.pallas_call(functools.partial(gather_kernel, n), out_shape=(jax.ShapeD...  46.7 us
    pallas_call x1, Pallas kernels, final(): pl.pallas_call(functools.partial(final_kernel, heads, n), out_shape=(jax....  35.7 us
    pallas_call x1, Pallas kernels, finish(): pl.pallas_call(functools.partial(finish_kernel, n, heads), out_shape=(jax...  6.08 us
  transfers between devices with their start and end apart: 4, of which 0 were waited for; matrix products, arithmetic and copies ran while one was open for 0% of the time, Pallas kernels for 80%

profile of v2, /device:TPU:0, one launch (start us, length us, event | category | flops | bytes accessed | tf_op | source)
XLA Modules:
  0.0 285.4 jit_solution(7027922696598668587)
XLA Ops:
  7.2 0.0 copy-start
  7.2 0.0 all-gather.4.cloned.1.call-start
  7.2 0.7 all-gather.4.cloned.1.call-update
  7.9 0.0 all-gather.6.cloned.1.call-start
  8.0 46.7 %gather_in.1 = (bf16[3072,768]{1,0:T(8,128)(2,1)}, bf16[8,96,576]{2,1,0:T(8,128)(2,1)}, bf16[4,96,768]{2,1,0:T(8,128)(2,1)}) custom-call(bf16[768,768]{1,0:T(8,128)(2,1)} %tok_ref.3, bf16[96,2304]{1,0:T(8,128)(2,1)} %weight_ref.1, bf16[96,3072]{1,0:T(8,128)(2,1)} %exp_ref.1), custom_call_target="tpu_custom_call" | custom-call | tf_op jit(solution)/shard_map/gather_in/pallas_call | solution.py:643
  54.7 0.0 all-gather.6.cloned.1.call-update
  54.7 0.0 all-gather.8.cloned.1.call-start
  54.8 0.7 all-gather.8.cloned.1.call-update
  55.5 0.0 reduce-scatter.2.cloned.1.call-start
  55.5 0.0 copy-done
  55.5 0.7 copy.42.lens_ref
  56.2 51.9 %attend.1 = (bf16[3,3072,64]{2,1,0:T(8,128)(2,1)}, bf16[3,3072,64]{2,1,0:T(8,128)(2,1)}, bf16[3,3072,64]{2,1,0:T(8,128)(2,1)}, bf16[3,6,64,512]{3,2,1,0:T(8,128)...) custom-call(s32[8,2]{1,0:T(8,128)} %copy.42.lens_ref, ...), custom_call_target="tpu_custom_call" | custom-call | flops 20434649088 | bytes 8257536 | tf_op jit(solution)/shard_map/attend/pallas_call | solution.py:218
  108.1 0.0 all-gather.4.cloned.1.call-done.wo_ref
  108.2 0.0 all-gather.6.cloned.1.call-done.wc_hbm
  108.2 47.0 %feed_forward.1 = (bf16[768,768]{1,0:T(8,128)(2,1)}, f32[768,768]{1,0:T(8,128)}, bf16[192,3072]{1,0:T(8,128)(2,1)}, f32[8,16,384]{2,1,0:T(8,128)}, bf16[3072,768...) custom-call(s32[8]{0:T(128)} %kept_ref.4, ...), custom_call_target="tpu_custom_call" | custom-call | flops 24461180928 | bytes 49545216 | tf_op jit(solution)/shard_map/feed_forward/pallas_call | solution.py:1123
  155.2 0.0 reduce-scatter.2.cloned.1.call-update
  155.3 81.7 %attend_back.1 = (bf16[3,4,192,768]{3,2,1,0:T(8,128)(2,1)}, bf16[8,96,576]{2,1,0:T(8,128)(2,1)}, bf16[96,768]{1,0:T(8,128)(2,1)}, bf16[96,192]{1,0:T(8,128)(2,1)}, f32[8,192]{1,0:T(8,128)}) custom-call(s32[8,2]{1,0:T(8,128)} %copy.42.lens_ref, s32[8]{0:T(128)} %kept_ref.5, f32[12]{0:T(128)} %gate_ref.5, s32[12]{0:T(128)} %mask_ref.5, ...), custom_call_target="tpu_custom_call" | custom-call | flops 47009759232 | bytes 15335424 | tf_op jit(solution)/shard_map/attend_back/pallas_call | solution.py:485
  237.0 0.0 all-gather.8.cloned.1.call-done.w_hbm
  237.0 0.0 reduce-scatter.2.cloned.1.call-done
  237.0 35.7 %final.1 = (f32[768,768]{1,0:T(8,128)}, bf16[4,96,768]{2,1,0:T(8,128)(2,1)}, bf16[4,96,192]{2,1,0:T(8,128)(2,1)}, bf16[4,96,768]{2,1,0:T(8,128)(2,1)}, bf16[4,96...) custom-call(f32[768,768]{1,0:T(8,128)} %get-tuple-element.77.base_hbm, ...), custom_call_target="tpu_custom_call" | custom-call | flops 2717908992 | bytes 3538944 | tf_op jit(solution)/shard_map/final/pallas_call | solution.py:774
  272.8 6.1 %finish.1 = (f32[4,96,768]{2,1,0:T(8,128)}, f32[96,3072]{1,0:T(8,128)}, f32[96,2304]{1,0:T(8,128)}, f32[768,768]{1,0:T(8,128)}, bf16[768,768]{1,0:T(8,128)(2,1)}...) custom-call(f32[12]{0:T(128)} %gate_ref.5, ...), custom_call_target="tpu_custom_call" | custom-call | tf_op jit(solution)/shard_map/finish/pallas_call | solution.py:880
Async XLA Ops:
  7.2 48.3 %copy-start = (s32[8,2]{0,1:T(2,128)S(1)}, s32[8,2]{0,1:T(2,128)}, u32[]{:S(2)}) copy-start(s32[8,2]{0,1:T(2,128)} %param.47) | copy-start | bytes 196
  7.2 101.0 %all-gather.4.cloned.1.call-start = ((), (), s32[]{:S(2)}) async-start(), calls=%async_computation.1 | async-start | bytes 1327104 | tf_op jit(solution)/shard_map/all_gather | solution.py:1218
  7.9 100.2 %all-gather.6.cloned.1.call-start = ((), (), s32[]{:S(2)}) async-start(), calls=%async_computation.2 | async-start | bytes 5308416 | tf_op jit(solution)/shard_map/all_gather | solution.py:1216
  54.7 182.3 %all-gather.8.cloned.1.call-start = ((), (), s32[]{:S(2)}) async-start(), calls=%async_computation.3 | async-start | bytes 3981312 | tf_op jit(solution)/shard_map/all_gather | solution.py:1217
  55.5 181.6 %reduce-scatter.2.cloned.1.call-start = ((), (), s32[]{:S(2)}) async-start(), calls=%async_computation.4 | async-start | bytes 5308416 | tf_op jit(solution)/shard_map/reduce_scatter | solution.py:1260
Sparse Core Ops, SparseCore 0:
  9.7 35.7 all-gather.3
  54.8 49.8 all-gather.5
  106.4 40.3 all-gather.7
  155.4 57.6 reduce-scatter.1

commit v3 on v2

--- a/solution.py
+++ b/solution.py
@@ -79,17 +79,22 @@
 
 
 def attend_kernel(
-    heads, n, lens_ref, kept_ref, gate_ref, mask_ref, qb_ref, vb_ref, tok_ref, w_ref, exp_ref,
+    heads, n, lens_ref, kept_ref, gate_ref, mask_ref, qb_ref, vb_ref, tok_hbm, w_hbm, exp_ref,
     q_sc, k_sc, v_ref, kt_ref, ctx_ref, lse_ref, full_ref, exp_all,
-    vt_sc, ct_sc, vec_ref, exp_buf,
+    tok_ref, w_ref, vt_sc, ct_sc, vec_ref, exp_buf,
     local_sem, s_sem, r_sem, s_e, r_e,
 ):
     s, w = lax.axis_index("seq"), lax.axis_index("wt")
     others = [flip(s, k) for k in (1, 2, 3)]
     mate = (s, flip(w, 1))
     short_first = lens_ref[w, 0] == SHORT
+    operands = [
+        pltpu.make_async_copy(tok_hbm, tok_ref, local_sem.at[heads + 1]),
+        pltpu.make_async_copy(w_hbm, w_ref, local_sem.at[heads + 2]),
+    ]
     come = pltpu.make_async_copy(exp_ref, exp_buf, local_sem.at[heads])
-    come.start()
+    for copy in operands + [come]:
+        copy.start()
     meet([(p, w) for p in others] + [mate])
     core, quarter = lax.rem(w, 2), exp_ref.shape[2]
 
@@ -122,6 +127,8 @@
     come.wait()
     own_part = pltpu.make_async_copy(exp_buf, exp_place(s), local_sem.at[heads])
     own_part.start()
+    for copy in operands:
+        copy.wait()
 
     def project(i, carry):
         rows = pl.ds(pl.multiple_of(i * TQ, TQ), TQ)
@@ -227,14 +234,16 @@
             jax.ShapeDtypeStruct((4 * HD * heads, GLEN // 4), bf16),
             jax.ShapeDtypeStruct((n // 2, 2, exp_part.shape[1], 4 * exp_part.shape[2]), bf16),
         ),
-        in_specs=[IN_SMEM] * 4 + [IN_VMEM] * 4 + [ANYWHERE],
+        in_specs=[IN_SMEM] * 4 + [IN_VMEM] * 2 + [ANYWHERE] * 3,
         out_specs=(IN_VMEM,) * 6 + (ANYWHERE, ANYWHERE),
         scratch_shapes=[
+            pltpu.VMEM((GLEN // TQ, TQ, tokens_all.shape[1]), bf16),
+            pltpu.VMEM(weight.shape, bf16),
             pltpu.VMEM((heads, HD, GLEN), bf16),
             pltpu.VMEM((GLEN // TQ, HD, TQ), bf16),
             pltpu.VMEM((2, width), f32),
             pltpu.VMEM(exp_part.shape, bf16),
-            pltpu.SemaphoreType.DMA((heads + 1,)),
+            pltpu.SemaphoreType.DMA((heads + 3,)),
         ]
         + dma_sems(3 * heads)
         + dma_sems(7),
@@ -253,9 +262,9 @@
 
 def attend_back_kernel(
     heads, n, lens_ref, kept_ref, gate_ref, mask_ref, q_hbm, k_hbm, v_hbm, kt_hbm,
-    ctx_ref, gctx_ref, lse_ref, tok_hbm,
+    ctx_hbm, gctx_hbm, lse_hbm, tok_hbm,
     e_own_hbm, e_got_hbm, o_own_hbm, o_got_hbm, pieces_o, dw_o, exp_o, out_o, late_o,
-    tok_v, e_own, o_own, e_got, o_got, e_all, o_all, e_sum, o_sum, e_z, o_z, stage, late_sc, row_sc,
+    ctx_ref, gctx_ref, lse_ref, tok_v, e_own, o_own, e_got, o_got, e_all, o_all, e_sum, o_sum, e_z, o_z, stage, late_sc, row_sc,
     q_all, k_all, v_all, kt_all, g_sc, g_nat, delta_sc, delta_nat, dqt_sc, dk_sc, dv_sc, acc,
     l_in, l_out, s_p, r_p, s_e, r_e, s_z, r_z,
 ):
@@ -279,8 +288,11 @@
         pltpu.make_async_copy(o_own_hbm, o_own, l_in.at[4 * heads + 2]),
         pltpu.make_async_copy(o_got_hbm, o_got, l_in.at[4 * heads + 3]),
         pltpu.make_async_copy(tok_hbm, tok_v, l_in.at[4 * heads + 4]),
+        pltpu.make_async_copy(ctx_hbm, ctx_ref, l_in.at[4 * heads + 5]),
+        pltpu.make_async_copy(gctx_hbm, gctx_ref, l_in.at[4 * heads + 6]),
+        pltpu.make_async_copy(lse_hbm, lse_ref, l_in.at[4 * heads + 7]),
     ]
-    for copy in loads[:4] + taken(0):
+    for copy in loads[:4] + loads[5:] + taken(0):
         copy.start()
     for h in range(1, heads):
         for copy in taken(h):
@@ -321,6 +333,8 @@
     o_all[s] = o_got[s]
     late_sc[...] = jnp.zeros_like(late_sc)
     row_sc[...] = jnp.zeros_like(row_sc)
+    for copy in loads[5:]:
+        copy.wait()
     for h in range(heads):
         for copy in taken(h):
             copy.wait()
@@ -493,10 +507,12 @@
         ),
         in_specs=[IN_SMEM] * 4
         + [ANYWHERE] * 4
-        + [IN_VMEM, IN_VMEM, IN_VMEM, ANYWHERE]
-        + [ANYWHERE] * 4,
+        + [ANYWHERE] * 8,
         out_specs=(ANYWHERE, IN_VMEM, IN_VMEM, IN_VMEM, IN_VMEM),
         scratch_shapes=[
+            pltpu.VMEM(ctx.shape, bf16),
+            pltpu.VMEM(g.shape, bf16),
+            pltpu.VMEM(lse.shape, f32),
             pltpu.VMEM(tokens_all.shape, bf16),
         ]
         + quarters * 3
@@ -516,7 +532,7 @@
             pltpu.VMEM((blocks, TQ, HD), f32),
             pltpu.VMEM((blocks, TQ, HD), f32),
             pltpu.VMEM((width, d), f32),
-            pltpu.SemaphoreType.DMA((4 * heads + 5,)),
+            pltpu.SemaphoreType.DMA((4 * heads + 8,)),
             pltpu.SemaphoreType.DMA((heads,)),
         ]
         + dma_sems(3 * heads)
@@ -665,9 +681,9 @@
 
 
 def final_kernel(
-    heads, n, base_hbm, pieces_hbm, w_hbm, con_ref, out_ref, att_ref, exp_ref, vec_ref, late_ref,
+    heads, n, base_hbm, pieces_hbm, w_hbm, con_ref, att_ref, out_ref, exp_ref, vec_ref, late_ref,
     tok_o, g_con, g_out, g_exp, g_att, r_vec2, r_late2,
-    base_v, pieces_v, w_v, r_con, h_att, m_att, r_att, r_vec, r_late,
+    base_v, pieces_v, w_v, a_own, r_con, h_att, m_att, r_att, r_vec, r_late,
     l_in, *sems,
 ):
     s, w = lax.axis_index("seq"), lax.axis_index("wt")
@@ -683,7 +699,10 @@
         pltpu.make_async_copy(src, dst, l_in.at[k])
         for k, (src, dst) in enumerate(((pieces_hbm, pieces_v), (w_hbm, w_v), (base_hbm, base_v)))
     ]
-    for copy in loads:
+    first = [pltpu.make_async_copy(con_ref.at[s], r_con.at[s], l_in.at[3])] + [
+        pltpu.make_async_copy(att_ref.at[2 * k + c], a_own.at[k], l_in.at[4 + k]) for k in range(nz)
+    ]
+    for copy in first + loads:
         copy.start()
     meet(seq_peers + wt_peers)
     pair = [send(att_ref.at[2 * k + 1 - c], h_att.at[k], sem["pair"], k, mate) for k in range(nz)]
@@ -696,15 +715,16 @@
         for j in range(1, n)
     ]
     lates = [send(late_ref, r_late.at[w], sem["late"], j, p) for j, p in enumerate(wt_peers)]
-    r_con[s] = con_ref[s]
     g_exp[s] = exp_ref[...]
     r_vec[w] = vec_ref[w]
     r_late[w] = late_ref[...]
     g_out[s] = out_ref[...]
+    for copy in first:
+        copy.wait()
     for copy in pair:
         copy.wait_recv()
     for k in range(nz):
-        m_att[k] = (att_ref[2 * k + c].astype(f32) + h_att[k].astype(f32)).astype(bf16)
+        m_att[k] = (a_own[k].astype(f32) + h_att[k].astype(f32)).astype(bf16)
     atts = [send(m_att.at[k], r_att.at[z], sem["att"], j, (s, 2 * k + c)) for j, k in enumerate(far)]
     r_att[z] = m_att[z]
     for copy in loads:
@@ -765,7 +785,7 @@
         copy.wait_send()
 
 
-def final(n, base, pieces, weight, con, out, att, exp_part, vec, late):
+def final(n, base, pieces, weight, con, att, out, exp_part, vec, late):
     heads = pieces.shape[0]
     r, d = con.shape[1:]
     cols = att.shape[2]
@@ -782,19 +802,20 @@
             jax.ShapeDtypeStruct((4,) + vec.shape[1:], f32),
             jax.ShapeDtypeStruct((4,) + late.shape, f32),
         ),
-        in_specs=[ANYWHERE] * 3 + [IN_VMEM] * 6,
+        in_specs=[ANYWHERE] * 5 + [IN_VMEM] * 4,
         out_specs=(IN_VMEM,) * 7,
         scratch_shapes=[
             pltpu.VMEM(base.shape, f32),
             pltpu.VMEM(pieces.shape, bf16),
             pltpu.VMEM(weight.shape, bf16),
+            pltpu.VMEM((nz, r, cols), bf16),
             pltpu.VMEM((4, r, d), bf16),
             pltpu.VMEM((nz, r, cols), bf16),
             pltpu.VMEM((nz, r, cols), bf16),
             pltpu.VMEM((nz, r, cols), bf16),
             pltpu.VMEM((n,) + vec.shape[1:], f32),
             pltpu.VMEM((n,) + late.shape, f32),
-            pltpu.SemaphoreType.DMA((3,)),
+            pltpu.SemaphoreType.DMA((4 + nz,)),
         ]
         + [sem for count in counts for sem in dma_sems(count)],
         compiler_params=remote_params(3),
@@ -802,7 +823,7 @@
             flops=8 * base.shape[0] * d * cols, bytes_accessed=8 * d * cols, transcendentals=0
         ),
         name="final",
-    )(base, pieces, weight, con, out, att, exp_part, vec, late)
+    )(base, pieces, weight, con, att, out, exp_part, vec, late)
 
 
 def finish_kernel(n, heads, gate_ref, mask_ref, *refs):
@@ -1280,8 +1301,8 @@
         pieces,
         full_attention,
         con_piece.reshape(seq_count, own_wide, model_width),
+        projection_grad,
         out_part,
-        projection_grad,
         exp_part,
         vec_sums,
         late_sums,

time: 286 us -> 282 us (0.986)
  Pallas kernels: 269 us -> 265 us
where the time goes in v3:
time: 282 us; the launch traced here: 281 us
  Pallas kernels  265 us (94%)
  between operations  13.9 us (5%)
    pallas_call x1, Pallas kernels, attend_back(): pl.pallas_call(functools.partial(attend_back_kernel, heads, n), out_shape...  80.7 us
    pallas_call x1, Pallas kernels, attend(): pl.pallas_call(functools.partial(attend_kernel, heads, n), out_shape=(jax...  50.1 us
    pallas_call x1, Pallas kernels, gather_in(): pl.pallas_call(functools.partial(gather_kernel, n), out_shape=(jax.ShapeD...  46.7 us
    pallas_call x1, Pallas kernels, feed_forward(): pl.pallas_call(functools.partial(feed_forward_kernel, steps, chunk), out_...  46.5 us
    pallas_call x1, Pallas kernels, final(): pl.pallas_call(functools.partial(final_kernel, heads, n), out_shape=(jax....  35.2 us
    pallas_call x1, Pallas kernels, finish(): pl.pallas_call(functools.partial(finish_kernel, n, heads), out_shape=(jax...  6.08 us
  transfers between devices with their start and end apart: 4, of which 0 were waited for; matrix products, arithmetic and copies ran while one was open for 0% of the time, Pallas kernels for 80%

profile of v3, /device:TPU:0, one launch (start us, length us, event | category | flops | bytes accessed | tf_op | source)
XLA Modules:
  0.0 281.5 jit_solution(2017698698110127361)
XLA Ops:
  7.2 0.0 copy-start
  7.2 0.0 all-gather.4.cloned.1.call-start
  7.2 0.7 all-gather.4.cloned.1.call-update
  7.9 0.0 all-gather.6.cloned.1.call-start
  8.0 46.7 %gather_in.1 = (bf16[3072,768]{1,0:T(8,128)(2,1)}, bf16[8,96,576]{2,1,0:T(8,128)(2,1)}, bf16[4,96,768]{2,1,0:T(8,128)(2,1)}) custom-call(bf16[768,768]{1,0:T(8,128)(2,1)} %tok_ref.3, bf16[96,2304]{1,0:T(8,128)(2,1)} %weight_ref.1, bf16[96,3072]{1,0:T(8,128)(2,1)} %exp_ref.1), custom_call_target="tpu_custom_call" | custom-call | tf_op jit(solution)/shard_map/gather_in/pallas_call | solution.py:659
  54.7 0.0 all-gather.6.cloned.1.call-update
  54.7 0.0 all-gather.8.cloned.1.call-start
  54.8 0.7 all-gather.8.cloned.1.call-update
  55.5 0.0 reduce-scatter.2.cloned.1.call-start
  55.5 0.0 copy-done
  55.5 0.7 copy.42.lens_ref
  56.2 50.1 %attend.1 = (bf16[3,3072,64]{2,1,0:T(8,128)(2,1)}, bf16[3,3072,64]{2,1,0:T(8,128)(2,1)}, bf16[3,3072,64]{2,1,0:T(8,128)(2,1)}, bf16[3,6,64,512]{3,2,1,0:T(8,128)...) custom-call(s32[8,2]{1,0:T(8,128)} %copy.42.lens_ref, ...), custom_call_target="tpu_custom_call" | custom-call | flops 20434649088 | bytes 8257536 | tf_op jit(solution)/shard_map/attend/pallas_call | solution.py:225
  106.3 0.0 all-gather.4.cloned.1.call-done.wo_ref
  106.3 0.0 all-gather.6.cloned.1.call-done.wc_hbm
  106.3 46.5 %feed_forward.1 = (bf16[768,768]{1,0:T(8,128)(2,1)}, f32[768,768]{1,0:T(8,128)}, bf16[192,3072]{1,0:T(8,128)(2,1)}, f32[8,16,384]{2,1,0:T(8,128)}, bf16[3072,768...) custom-call(s32[8]{0:T(128)} %kept_ref.4, ...), custom_call_target="tpu_custom_call" | custom-call | flops 24461180928 | bytes 49545216 | tf_op jit(solution)/shard_map/feed_forward/pallas_call | solution.py:1144
  152.9 0.0 reduce-scatter.2.cloned.1.call-update
  152.9 80.7 %attend_back.1 = (bf16[3,4,192,768]{3,2,1,0:T(8,128)(2,1)}, bf16[8,96,576]{2,1,0:T(8,128)(2,1)}, bf16[96,768]{1,0:T(8,128)(2,1)}, bf16[96,192]{1,0:T(8,128)(2,1)}, f32[8,192]{1,0:T(8,128)}) custom-call(s32[8,2]{1,0:T(8,128)} %copy.42.lens_ref, s32[8]{0:T(128)} %kept_ref.5, f32[12]{0:T(128)} %gate_ref.5, s32[12]{0:T(128)} %mask_ref.5, ...), custom_call_target="tpu_custom_call" | custom-call | flops 47009759232 | bytes 15335424 | tf_op jit(solution)/shard_map/attend_back/pallas_call | solution.py:499
  233.6 0.0 all-gather.8.cloned.1.call-done.w_hbm
  233.6 0.0 reduce-scatter.2.cloned.1.call-done
  233.6 35.2 %final.1 = (f32[768,768]{1,0:T(8,128)}, bf16[4,96,768]{2,1,0:T(8,128)(2,1)}, bf16[4,96,192]{2,1,0:T(8,128)(2,1)}, bf16[4,96,768]{2,1,0:T(8,128)(2,1)}, bf16[4,96...) custom-call(f32[768,768]{1,0:T(8,128)} %get-tuple-element.77.base_hbm, ...), custom_call_target="tpu_custom_call" | custom-call | flops 2717908992 | bytes 3538944 | tf_op jit(solution)/shard_map/final/pallas_call | solution.py:794
  268.9 6.1 %finish.1 = (f32[4,96,768]{2,1,0:T(8,128)}, f32[96,3072]{1,0:T(8,128)}, f32[96,2304]{1,0:T(8,128)}, f32[768,768]{1,0:T(8,128)}, bf16[768,768]{1,0:T(8,128)(2,1)}...) custom-call(f32[12]{0:T(128)} %gate_ref.5, ...), custom_call_target="tpu_custom_call" | custom-call | tf_op jit(solution)/shard_map/finish/pallas_call | solution.py:901
Async XLA Ops:
  7.2 48.3 %copy-start = (s32[8,2]{0,1:T(2,128)S(1)}, s32[8,2]{0,1:T(2,128)}, u32[]{:S(2)}) copy-start(s32[8,2]{0,1:T(2,128)} %param.47) | copy-start | bytes 196
  7.2 99.1 %all-gather.4.cloned.1.call-start = ((), (), s32[]{:S(2)}) async-start(), calls=%async_computation.1 | async-start | bytes 1327104 | tf_op jit(solution)/shard_map/all_gather | solution.py:1239
  7.9 98.4 %all-gather.6.cloned.1.call-start = ((), (), s32[]{:S(2)}) async-start(), calls=%async_computation.2 | async-start | bytes 5308416 | tf_op jit(solution)/shard_map/all_gather | solution.py:1237
  54.7 178.8 %all-gather.8.cloned.1.call-start = ((), (), s32[]{:S(2)}) async-start(), calls=%async_computation.3 | async-start | bytes 3981312 | tf_op jit(solution)/shard_map/all_gather | solution.py:1238
  55.5 178.1 %reduce-scatter.2.cloned.1.call-start = ((), (), s32[]{:S(2)}) async-start(), calls=%async_computation.4 | async-start | bytes 5308416 | tf_op jit(solution)/shard_map/reduce_scatter | solution.py:1281
Sparse Core Ops, SparseCore 0:
  9.7 35.7 all-gather.3
  54.8 49.8 all-gather.5
  106.4 40.9 all-gather.7
  153.0 59.1 reduce-scatter.1

commit v4 on v3

--- a/solution.py
+++ b/solution.py
@@ -80,8 +80,8 @@
 
 def attend_kernel(
     heads, n, lens_ref, kept_ref, gate_ref, mask_ref, qb_ref, vb_ref, tok_hbm, w_hbm, exp_ref,
-    q_sc, k_sc, v_ref, kt_ref, ctx_ref, lse_ref, full_ref, exp_all,
-    tok_ref, w_ref, vt_sc, ct_sc, vec_ref, exp_buf,
+    q_o, k_o, v_o, kt_o, ctx_ref, lse_ref, full_ref, exp_all,
+    tok_ref, w_ref, q_sc, k_sc, v_ref, kt_ref, vt_sc, ct_sc, vec_ref, exp_buf,
     local_sem, s_sem, r_sem, s_e, r_e,
 ):
     s, w = lax.axis_index("seq"), lax.axis_index("wt")
@@ -146,6 +146,12 @@
         return carry
 
     lax.fori_loop(0, GLEN // TQ, project, 0)
+    handed = [
+        pltpu.make_async_copy(src, dst, local_sem.at[heads + 3 + k])
+        for k, (src, dst) in enumerate(((q_sc, q_o), (k_sc, k_o), (v_ref, v_o), (kt_ref, kt_o)))
+    ]
+    for copy in handed:
+        copy.start()
 
     def leaving(h):
         rows = pl.ds(pl.multiple_of(h * HD, HD), HD)
@@ -207,6 +213,8 @@
         return carry
 
     lax.fori_loop(0, heads, one_head, 0)
+    for copy in handed:
+        copy.wait()
     own_part.wait()
     spread[3].wait_recv()
     for _, copy in passed:
@@ -235,15 +243,19 @@
             jax.ShapeDtypeStruct((n // 2, 2, exp_part.shape[1], 4 * exp_part.shape[2]), bf16),
         ),
         in_specs=[IN_SMEM] * 4 + [IN_VMEM] * 2 + [ANYWHERE] * 3,
-        out_specs=(IN_VMEM,) * 6 + (ANYWHERE, ANYWHERE),
+        out_specs=(ANYWHERE,) * 4 + (IN_VMEM,) * 2 + (ANYWHERE, ANYWHERE),
         scratch_shapes=[
             pltpu.VMEM((GLEN // TQ, TQ, tokens_all.shape[1]), bf16),
             pltpu.VMEM(weight.shape, bf16),
+            pltpu.VMEM((heads, GLEN, HD), bf16),
+            pltpu.VMEM((heads, GLEN, HD), bf16),
+            pltpu.VMEM((heads, GLEN, HD), bf16),
+            pltpu.VMEM((heads, GLEN // TQ, HD, TQ), bf16),
             pltpu.VMEM((heads, HD, GLEN), bf16),
             pltpu.VMEM((GLEN // TQ, HD, TQ), bf16),
             pltpu.VMEM((2, width), f32),
             pltpu.VMEM(exp_part.shape, bf16),
-            pltpu.SemaphoreType.DMA((heads + 3,)),
+            pltpu.SemaphoreType.DMA((heads + 7,)),
         ]
         + dma_sems(3 * heads)
         + dma_sems(7),
@@ -682,8 +694,8 @@
 
 def final_kernel(
     heads, n, base_hbm, pieces_hbm, w_hbm, con_ref, att_ref, out_ref, exp_ref, vec_ref, late_ref,
-    tok_o, g_con, g_out, g_exp, g_att, r_vec2, r_late2,
-    base_v, pieces_v, w_v, a_own, r_con, h_att, m_att, r_att, r_vec, r_late,
+    tok_hbm, g_con, g_out, g_exp, g_att, r_vec2, r_late2,
+    tok_o, base_v, pieces_v, w_v, a_own, r_con, h_att, m_att, r_att, r_vec, r_late,
     l_in, *sems,
 ):
     s, w = lax.axis_index("seq"), lax.axis_index("wt")
@@ -745,6 +757,10 @@
         for ref, name in zip(own, ("con2", "vec2", "late2", "att2"), strict=True)
     )
 
+    def given(i):
+        there = pl.ds(pl.multiple_of(i * block, block), block)
+        return pltpu.make_async_copy(tok_o.at[there], tok_hbm.at[there], l_in.at[4 + nz + i])
+
     def tokens_block(i, carry):
         there = pl.ds(pl.multiple_of(i * block, block), block)
         total = base_v[there, :]
@@ -753,6 +769,7 @@
                 at = (heads * k + h) * cols
                 total = total + mm(pieces_v[h, k, :, there].T, w_v[:, at : at + cols], NT)
         tok_o[there, :] = total
+        given(i).start()
 
         @pl.when(i == 0)
         def _():
@@ -779,6 +796,8 @@
         return carry
 
     lax.fori_loop(0, 3, tokens_block, 0)
+    for i in range(3):
+        given(i).wait()
     for copy in out2 + con2 + vec2 + late2 + exp2 + att2:
         copy.wait_recv()
     for copy in pair + cons + vecs + lates + atts + con2 + vec2 + late2 + exp2 + out2 + att2:
@@ -803,8 +822,9 @@
             jax.ShapeDtypeStruct((4,) + late.shape, f32),
         ),
         in_specs=[ANYWHERE] * 5 + [IN_VMEM] * 4,
-        out_specs=(IN_VMEM,) * 7,
+        out_specs=(ANYWHERE,) + (IN_VMEM,) * 6,
         scratch_shapes=[
+            pltpu.VMEM(base.shape, f32),
             pltpu.VMEM(base.shape, f32),
             pltpu.VMEM(pieces.shape, bf16),
             pltpu.VMEM(weight.shape, bf16),
@@ -815,7 +835,7 @@
             pltpu.VMEM((nz, r, cols), bf16),
             pltpu.VMEM((n,) + vec.shape[1:], f32),
             pltpu.VMEM((n,) + late.shape, f32),
-            pltpu.SemaphoreType.DMA((4 + nz,)),
+            pltpu.SemaphoreType.DMA((7 + nz,)),
         ]
         + [sem for count in counts for sem in dma_sems(count)],
         compiler_params=remote_params(3),

time: 282 us -> 280 us (level)
  transfers between devices with their start and end apart: 4 -> 4, of which waited for: 0 -> 1; matrix products, arithmetic and copies ran while one was open for 0% -> 0% of each run, Pallas kernels for 80% -> 79%
where the time goes in v4:
time: 280 us
  Pallas kernels  263 us (94%)
  between operations  13.9 us (5%)
    pallas_call x1, Pallas kernels, attend_back(): pl.pallas_call(functools.partial(attend_back_kernel, heads, n), out_shape...  81.5 us
    pallas_call x1, Pallas kernels, attend(): pl.pallas_call(functools.partial(attend_kernel, heads, n), out_shape=(jax...  47.5 us
    pallas_call x1, Pallas kernels, gather_in(): pl.pallas_call(functools.partial(gather_kernel, n), out_shape=(jax.ShapeD...  46.7 us
    pallas_call x1, Pallas kernels, feed_forward(): pl.pallas_call(functools.partial(feed_forward_kernel, steps, chunk), out_...  46.5 us
    pallas_call x1, Pallas kernels, final(): pl.pallas_call(functools.partial(final_kernel, heads, n), out_shape=(jax....  34.5 us
    pallas_call x1, Pallas kernels, finish(): pl.pallas_call(functools.partial(finish_kernel, n, heads), out_shape=(jax...  6.08 us
  transfers between devices with their start and end apart: 4, of which 1 were waited for; matrix products, arithmetic and copies ran while one was open for 0% of the time, Pallas kernels for 79%

profile of v4, /device:TPU:0, one launch (start us, length us, event | category | flops | bytes accessed | tf_op | source)
XLA Modules:
  0.0 280.0 jit_solution(7369198662367957047)
XLA Ops:
  7.2 0.0 copy-start
  7.2 0.0 all-gather.4.cloned.1.call-start
  7.2 0.7 all-gather.4.cloned.1.call-update
  7.9 0.0 all-gather.6.cloned.1.call-start
  8.0 46.7 %gather_in.1 = (bf16[3072,768]{1,0:T(8,128)(2,1)}, bf16[8,96,576]{2,1,0:T(8,128)(2,1)}, bf16[4,96,768]{2,1,0:T(8,128)(2,1)}) custom-call(bf16[768,768]{1,0:T(8,128)(2,1)} %tok_ref.3, bf16[96,2304]{1,0:T(8,128)(2,1)} %weight_ref.1, bf16[96,3072]{1,0:T(8,128)(2,1)} %exp_ref.1), custom_call_target="tpu_custom_call" | custom-call | tf_op jit(solution)/shard_map/gather_in/pallas_call | solution.py:671
  54.7 0.0 all-gather.6.cloned.1.call-update
  54.7 0.0 all-gather.8.cloned.1.call-start
  54.8 0.7 all-gather.8.cloned.1.call-update
  55.5 0.0 reduce-scatter.2.cloned.1.call-start
  55.5 0.0 copy-done
  55.5 0.7 copy.42.lens_ref
  56.2 47.5 %attend.1 = (bf16[3,3072,64]{2,1,0:T(8,128)(2,1)}, bf16[3,3072,64]{2,1,0:T(8,128)(2,1)}, bf16[3,3072,64]{2,1,0:T(8,128)(2,1)}, bf16[3,6,64,512]{3,2,1,0:T(8,128)...) custom-call(s32[8,2]{1,0:T(8,128)} %copy.42.lens_ref, ...), custom_call_target="tpu_custom_call" | custom-call | flops 20434649088 | bytes 8257536 | tf_op jit(solution)/shard_map/attend/pallas_call | solution.py:233
  103.7 0.0 all-gather.4.cloned.1.call-done.wo_ref
  103.8 1.0 all-gather.6.cloned.1.call-done.wc_hbm
  104.8 46.5 %feed_forward.1 = (bf16[768,768]{1,0:T(8,128)(2,1)}, f32[768,768]{1,0:T(8,128)}, bf16[192,3072]{1,0:T(8,128)(2,1)}, f32[8,16,384]{2,1,0:T(8,128)}, bf16[3072,768...) custom-call(s32[8]{0:T(128)} %kept_ref.4, ...), custom_call_target="tpu_custom_call" | custom-call | flops 24461180928 | bytes 49545216 | tf_op jit(solution)/shard_map/feed_forward/pallas_call | solution.py:1164
  151.3 0.0 reduce-scatter.2.cloned.1.call-update
  151.3 81.5 %attend_back.1 = (bf16[3,4,192,768]{3,2,1,0:T(8,128)(2,1)}, bf16[8,96,576]{2,1,0:T(8,128)(2,1)}, bf16[96,768]{1,0:T(8,128)(2,1)}, bf16[96,192]{1,0:T(8,128)(2,1)}, f32[8,192]{1,0:T(8,128)}) custom-call(s32[8,2]{1,0:T(8,128)} %copy.42.lens_ref, s32[8]{0:T(128)} %kept_ref.5, f32[12]{0:T(128)} %gate_ref.5, s32[12]{0:T(128)} %mask_ref.5, ...), custom_call_target="tpu_custom_call" | custom-call | flops 47009759232 | bytes 15335424 | tf_op jit(solution)/shard_map/attend_back/pallas_call | solution.py:511
  232.8 0.0 all-gather.8.cloned.1.call-done.w_hbm
  232.9 0.0 reduce-scatter.2.cloned.1.call-done
  232.9 34.5 %final.1 = (f32[768,768]{1,0:T(8,128)}, bf16[4,96,768]{2,1,0:T(8,128)(2,1)}, bf16[4,96,192]{2,1,0:T(8,128)(2,1)}, bf16[4,96,768]{2,1,0:T(8,128)(2,1)}, bf16[4,96...) custom-call(f32[768,768]{1,0:T(8,128)} %get-tuple-element.77.base_hbm, ...), custom_call_target="tpu_custom_call" | custom-call | flops 2717908992 | bytes 3538944 | tf_op jit(solution)/shard_map/final/pallas_call | solution.py:813
  267.4 6.1 %finish.1 = (f32[4,96,768]{2,1,0:T(8,128)}, f32[96,3072]{1,0:T(8,128)}, f32[96,2304]{1,0:T(8,128)}, f32[768,768]{1,0:T(8,128)}, bf16[768,768]{1,0:T(8,128)(2,1)}...) custom-call(f32[12]{0:T(128)} %gate_ref.5, ...), custom_call_target="tpu_custom_call" | custom-call | tf_op jit(solution)/shard_map/finish/pallas_call | solution.py:921
Async XLA Ops:
  7.2 48.3 %copy-start = (s32[8,2]{0,1:T(2,128)S(1)}, s32[8,2]{0,1:T(2,128)}, u32[]{:S(2)}) copy-start(s32[8,2]{0,1:T(2,128)} %param.47) | copy-start | bytes 196
  7.2 96.6 %all-gather.4.cloned.1.call-start = ((), (), s32[]{:S(2)}) async-start(), calls=%async_computation.1 | async-start | bytes 1327104 | tf_op jit(solution)/shard_map/all_gather | solution.py:1259
  7.9 96.8 %all-gather.6.cloned.1.call-start = ((), (), s32[]{:S(2)}) async-start(), calls=%async_computation.2 | async-start | bytes 5308416 | tf_op jit(solution)/shard_map/all_gather | solution.py:1257
  54.7 178.1 %all-gather.8.cloned.1.call-start = ((), (), s32[]{:S(2)}) async-start(), calls=%async_computation.3 | async-start | bytes 3981312 | tf_op jit(solution)/shard_map/all_gather | solution.py:1258
  55.5 177.4 %reduce-scatter.2.cloned.1.call-start = ((), (), s32[]{:S(2)}) async-start(), calls=%async_computation.4 | async-start | bytes 5308416 | tf_op jit(solution)/shard_map/reduce_scatter | solution.py:1301
Sparse Core Ops, SparseCore 0:
  9.7 35.7 all-gather.3
  54.8 49.8 all-gather.5
  106.4 40.3 all-gather.7
  151.4 61.4 reduce-scatter.1

commit v5 on v4

--- a/solution.py
+++ b/solution.py
@@ -80,8 +80,8 @@
 
 def attend_kernel(
     heads, n, lens_ref, kept_ref, gate_ref, mask_ref, qb_ref, vb_ref, tok_hbm, w_hbm, exp_ref,
-    q_o, k_o, v_o, kt_o, ctx_ref, lse_ref, full_ref, exp_all,
-    tok_ref, w_ref, q_sc, k_sc, v_ref, kt_ref, vt_sc, ct_sc, vec_ref, exp_buf,
+    q_o, k_o, v_o, kt_o, ctx_o, lse_ref, full_ref, exp_all,
+    ctx_ref, tok_ref, w_ref, q_sc, k_sc, v_ref, kt_ref, vt_sc, ct_sc, vec_ref, exp_buf,
     local_sem, s_sem, r_sem, s_e, r_e,
 ):
     s, w = lax.axis_index("seq"), lax.axis_index("wt")
@@ -152,6 +152,10 @@
     ]
     for copy in handed:
         copy.start()
+
+    def stays(h):
+        rows = pl.ds(pl.multiple_of(h * HD, HD), HD)
+        return pltpu.make_async_copy(ctx_ref.at[rows], ctx_o.at[rows], local_sem.at[heads + 7 + h])
 
     def leaving(h):
         rows = pl.ds(pl.multiple_of(h * HD, HD), HD)
@@ -210,6 +214,7 @@
         for copy in copies:
             copy.start()
         own.start()
+        stays(h).start()
         return carry
 
     lax.fori_loop(0, heads, one_head, 0)
@@ -222,6 +227,7 @@
     for copy in spread:
         copy.wait_send()
     for h in range(heads):
+        stays(h).wait()
         copies, own = leaving(h)
         own.wait()
         for copy in copies:
@@ -243,8 +249,9 @@
             jax.ShapeDtypeStruct((n // 2, 2, exp_part.shape[1], 4 * exp_part.shape[2]), bf16),
         ),
         in_specs=[IN_SMEM] * 4 + [IN_VMEM] * 2 + [ANYWHERE] * 3,
-        out_specs=(ANYWHERE,) * 4 + (IN_VMEM,) * 2 + (ANYWHERE, ANYWHERE),
+        out_specs=(ANYWHERE,) * 5 + (IN_VMEM,) + (ANYWHERE, ANYWHERE),
         scratch_shapes=[
+            pltpu.VMEM((HD * heads, GLEN), bf16),
             pltpu.VMEM((GLEN // TQ, TQ, tokens_all.shape[1]), bf16),
             pltpu.VMEM(weight.shape, bf16),
             pltpu.VMEM((heads, GLEN, HD), bf16),
@@ -255,7 +262,7 @@
             pltpu.VMEM((GLEN // TQ, HD, TQ), bf16),
             pltpu.VMEM((2, width), f32),
             pltpu.VMEM(exp_part.shape, bf16),
-            pltpu.SemaphoreType.DMA((heads + 7,)),
+            pltpu.SemaphoreType.DMA((2 * heads + 7,)),
         ]
         + dma_sems(3 * heads)
         + dma_sems(7),
@@ -856,8 +863,8 @@
         pltpu.make_async_copy(src, dst, l_in.at[k])
         for k, (src, dst) in enumerate(zip(sources, inside, strict=True))
     ]
-    for copy in loads:
-        copy.start()
+    for k in (3, 4, 0, 1, 2, 5, 6, 7):
+        loads[k].start()
     outside = ((con_f, con_o), (exp_f, exp_o), (att_f, att_o), (tok_v, tok_o), (low_v, low_o))
     stores = [pltpu.make_async_copy(src, dst, l_out.at[k]) for k, (src, dst) in enumerate(outside)]
 
@@ -865,6 +872,9 @@
         return (parts[0] + parts[1]) + (parts[2] + parts[3])
 
     wide, cols, part = exp_v.shape[2], att_v.shape[2], out_v.shape[2]
+    for k in (3, 4):
+        loads[k].wait()
+        stores[k].start()
     loads[0].wait()
     con_f[...] = con_v[...].astype(f32)
     stores[0].start()
@@ -876,9 +886,6 @@
     for k in range(4):
         att_f[:, k * cols : (k + 1) * cols] = att_v[k].astype(f32)
     stores[2].start()
-    for k in (3, 4):
-        loads[k].wait()
-        stores[k].start()
     for copy in loads[5:]:
         copy.wait()
     for k in range(4):

time: 280 us -> 280 us (level)
  no operation moved by 1% of the time
where the time goes in v5:
time: 280 us
  Pallas kernels  262 us (94%)
  between operations  13.9 us (5%)
  waiting for transfers between devices  2.87 us (1%)
    pallas_call x1, Pallas kernels, attend_back(): pl.pallas_call(functools.partial(attend_back_kernel, heads, n), out_shape...  81.5 us
    pallas_call x1, Pallas kernels, attend(): pl.pallas_call(functools.partial(attend_kernel, heads, n), out_shape=(jax...  47.1 us
    pallas_call x1, Pallas kernels, gather_in(): pl.pallas_call(functools.partial(gather_kernel, n), out_shape=(jax.ShapeD...  46.7 us
    pallas_call x1, Pallas kernels, feed_forward(): pl.pallas_call(functools.partial(feed_forward_kernel, steps, chunk), out_...  46.5 us
    pallas_call x1, Pallas kernels, final(): pl.pallas_call(functools.partial(final_kernel, heads, n), out_shape=(jax....  34.5 us
    pallas_call x1, Pallas kernels, finish(): pl.pallas_call(functools.partial(finish_kernel, n, heads), out_shape=(jax...  6.05 us
  transfers between devices with their start and end apart: 4, of which 1 were waited for; matrix products, arithmetic and copies ran while one was open for 0% of the time, Pallas kernels for 79%

profile of v5, /device:TPU:0, one launch (start us, length us, event | category | flops | bytes accessed | tf_op | source)
XLA Modules:
  0.0 280.0 jit_solution(15637146422787425532)
XLA Ops:
  7.2 0.0 copy-start
  7.2 0.0 all-gather.4.cloned.1.call-start
  7.2 0.7 all-gather.4.cloned.1.call-update
  7.9 0.0 all-gather.6.cloned.1.call-start
  8.0 46.7 %gather_in.1 = (bf16[3072,768]{1,0:T(8,128)(2,1)}, bf16[8,96,576]{2,1,0:T(8,128)(2,1)}, bf16[4,96,768]{2,1,0:T(8,128)(2,1)}) custom-call(bf16[768,768]{1,0:T(8,128)(2,1)} %tok_ref.3, bf16[96,2304]{1,0:T(8,128)(2,1)} %weight_ref.1, bf16[96,3072]{1,0:T(8,128)(2,1)} %exp_ref.1), custom_call_target="tpu_custom_call" | custom-call | tf_op jit(solution)/shard_map/gather_in/pallas_call | solution.py:678
  54.7 0.0 all-gather.6.cloned.1.call-update
  54.7 0.0 all-gather.8.cloned.1.call-start
  54.8 0.7 all-gather.8.cloned.1.call-update
  55.5 0.0 reduce-scatter.2.cloned.1.call-start
  55.5 0.0 copy-done
  55.5 0.7 copy.42.lens_ref
  56.2 47.1 %attend.1 = (bf16[3,3072,64]{2,1,0:T(8,128)(2,1)}, bf16[3,3072,64]{2,1,0:T(8,128)(2,1)}, bf16[3,3072,64]{2,1,0:T(8,128)(2,1)}, bf16[3,6,64,512]{3,2,1,0:T(8,128)...) custom-call(s32[8,2]{1,0:T(8,128)} %copy.42.lens_ref, ...), custom_call_target="tpu_custom_call" | custom-call | flops 20434649088 | bytes 8257536 | tf_op jit(solution)/shard_map/attend/pallas_call | solution.py:239
  103.3 0.0 all-gather.4.cloned.1.call-done.wo_ref
  103.4 1.4 all-gather.6.cloned.1.call-done.wc_hbm
  104.8 46.5 %feed_forward.1 = (bf16[768,768]{1,0:T(8,128)(2,1)}, f32[768,768]{1,0:T(8,128)}, bf16[192,3072]{1,0:T(8,128)(2,1)}, f32[8,16,384]{2,1,0:T(8,128)}, bf16[3072,768...) custom-call(s32[8]{0:T(128)} %kept_ref.4, ...), custom_call_target="tpu_custom_call" | custom-call | flops 24461180928 | bytes 49545216 | tf_op jit(solution)/shard_map/feed_forward/pallas_call | solution.py:1171
  151.3 0.0 reduce-scatter.2.cloned.1.call-update
  151.3 81.5 %attend_back.1 = (bf16[3,4,192,768]{3,2,1,0:T(8,128)(2,1)}, bf16[8,96,576]{2,1,0:T(8,128)(2,1)}, bf16[96,768]{1,0:T(8,128)(2,1)}, bf16[96,192]{1,0:T(8,128)(2,1)}, f32[8,192]{1,0:T(8,128)}) custom-call(s32[8,2]{1,0:T(8,128)} %copy.42.lens_ref, s32[8]{0:T(128)} %kept_ref.5, f32[12]{0:T(128)} %gate_ref.5, s32[12]{0:T(128)} %mask_ref.5, ...), custom_call_target="tpu_custom_call" | custom-call | flops 47009759232 | bytes 15335424 | tf_op jit(solution)/shard_map/attend_back/pallas_call | solution.py:518
  232.8 0.0 all-gather.8.cloned.1.call-done.w_hbm
  232.9 0.0 reduce-scatter.2.cloned.1.call-done
  232.9 34.5 %final.1 = (f32[768,768]{1,0:T(8,128)}, bf16[4,96,768]{2,1,0:T(8,128)(2,1)}, bf16[4,96,192]{2,1,0:T(8,128)(2,1)}, bf16[4,96,768]{2,1,0:T(8,128)(2,1)}, bf16[4,96...) custom-call(f32[768,768]{1,0:T(8,128)} %get-tuple-element.77.base_hbm, ...), custom_call_target="tpu_custom_call" | custom-call | flops 2717908992 | bytes 3538944 | tf_op jit(solution)/shard_map/final/pallas_call | solution.py:820
  267.4 6.0 %finish.1 = (f32[4,96,768]{2,1,0:T(8,128)}, f32[96,3072]{1,0:T(8,128)}, f32[96,2304]{1,0:T(8,128)}, f32[768,768]{1,0:T(8,128)}, bf16[768,768]{1,0:T(8,128)(2,1)}...) custom-call(f32[12]{0:T(128)} %gate_ref.5, ...), custom_call_target="tpu_custom_call" | custom-call | tf_op jit(solution)/shard_map/finish/pallas_call | solution.py:928
Async XLA Ops:
  7.2 48.3 %copy-start = (s32[8,2]{0,1:T(2,128)S(1)}, s32[8,2]{0,1:T(2,128)}, u32[]{:S(2)}) copy-start(s32[8,2]{0,1:T(2,128)} %param.47) | copy-start | bytes 196
  7.2 96.1 %all-gather.4.cloned.1.call-start = ((), (), s32[]{:S(2)}) async-start(), calls=%async_computation.1 | async-start | bytes 1327104 | tf_op jit(solution)/shard_map/all_gather | solution.py:1266
  7.9 96.8 %all-gather.6.cloned.1.call-start = ((), (), s32[]{:S(2)}) async-start(), calls=%async_computation.2 | async-start | bytes 5308416 | tf_op jit(solution)/shard_map/all_gather | solution.py:1264
  54.7 178.1 %all-gather.8.cloned.1.call-start = ((), (), s32[]{:S(2)}) async-start(), calls=%async_computation.3 | async-start | bytes 3981312 | tf_op jit(solution)/shard_map/all_gather | solution.py:1265
  55.5 177.4 %reduce-scatter.2.cloned.1.call-start = ((), (), s32[]{:S(2)}) async-start(), calls=%async_computation.4 | async-start | bytes 5308416 | tf_op jit(solution)/shard_map/reduce_scatter | solution.py:1308
Sparse Core Ops, SparseCore 0:
  9.7 35.7 all-gather.3
  54.8 49.8 all-gather.5
  106.4 40.3 all-gather.7
  151.4 61.4 reduce-scatter.1
